TPU v7x, 128 devices: a whole 4x4x4 slice. The times are simulated.
128 devices in a mesh: region: 4 (over y), row: 8 (over z, x_hi), col: 4 (over x_lo, core).
Axes of the slice: x: 4 (x_hi: 2, x_lo: 2; x = x_hi * 2 + x_lo), y: 4, z: 4, core: 2. Of those that a mesh axis runs over, the one named last changes fastest.
Arguments:
- noisy_field: bfloat16 [4, 1024, 512, 128], P('region', 'row', 'col'), may hold values from -40 to 40
- coarse_cells: float32 [32768, 640], P(('region', 'row', 'col')), may hold values from -6 to 6
- coarse_proj: float32 [640, 128], replicated, may hold values from -0.25 to 0.25
- kernel_first: bfloat16 [3, 3, 128, 128], replicated, may hold values from -0.1875 to 0.1875
- kernel_second: bfloat16 [3, 3, 128, 128], replicated, may hold values from -0.1875 to 0.1875
- gain_first: float32 [128], replicated, may hold values from 0.25 to 1.75
- shift_first: float32 [128], replicated, may hold values from -3 to 3
- gain_second: float32 [128], replicated, may hold values from 0.25 to 1.75
- shift_second: float32 [128], replicated, may hold values from -3 to 3
- request_ids: int32 [4, 8, 4, 128, 6], P('region', 'row', 'col'), may hold values from 0 to 32767, as said below
- patch_slots: int32 [4, 8, 4, 169], P('region', 'row', 'col'), may hold values from 0 to 767, as said below
- tile_offsets: int32 [4, 8, 4, 2], P('region', 'row', 'col'), may hold values from 0 to 127
Outputs:
- denoised: bfloat16 [4, 1024, 512, 128], P('region', 'row', 'col')
Inputs may be any that keep to these rules, and one draw needn't show every extreme that they name: request_ids[r, i, j, o, m] is a cell of owner o: o * 256 <= value < (o + 1) * 256, owner o being the device of index o over region, row, col in that order. `patch_slots`: the 169 entries of one tile are distinct; in every draw one owner has all 6 of its entries used by every tile.
All inputs are finite; a program needn't handle non-finite values.
Results may differ from a plain program's by a relative error of at most 0.0051.
Values may be sent and summed in bfloat16 or wider, within the bound.
A program may use at most 64 MiB of HBM per device.

v0:
```python
import functools

import jax
import jax.numpy as jnp
from jax import lax
from jax.experimental import pallas as pl
from jax.experimental.pallas import tpu as pltpu
from jax.sharding import PartitionSpec as P

GROUPS = 32
STEP = 9
PATCH = 13
MOST = 6
TILE = 128
C = 128
CC = 640
HELD = 256
AXES = ("region", "row", "col")
MESH = pl.DeviceIdType.MESH
F32 = jnp.float32
BF16 = jnp.bfloat16
PAIRS = 4


def split3(x):
    hi = x.astype(BF16)
    rest = x - hi.astype(F32)
    mid = rest.astype(BF16)
    lo = (rest - mid.astype(F32)).astype(BF16)
    return hi, mid, lo


def cubic(distance):
    near_part = (1.5 * distance - 2.5) * distance * distance + 1.0
    far_part = ((-0.5 * distance + 2.5) * distance - 4.0) * distance + 2.0
    return jnp.where(distance < 1.0, near_part, jnp.where(distance < 2.0, far_part, 0.0))


def weight_terms(point, lane, offset):
    position = (offset.astype(F32) + point.astype(F32) * STEP) / 128.0 + 1.0
    cell = lane % 16
    group = lane // 16
    weight = cubic(jnp.abs(position - cell.astype(F32)))
    weight = jnp.where(cell < PATCH, weight, 0.0)
    hi, mid, lo = (t.astype(F32) for t in split3(weight))
    return jnp.where(group < 3, hi, jnp.where(group < 5, mid, jnp.where(group < 6, lo, 0.0)))


def silu(v):
    half = 0.5 * v
    return half + half * jnp.tanh(half)


def kernel(
    noisy_hbm,
    cells_hbm,
    proj_hbm,
    k1_hbm,
    k2_hbm,
    g1_ref,
    s1_ref,
    g2_ref,
    s2_ref,
    ids_ref,
    slots_ref,
    off_ref,
    out_hbm,
    noisy,
    cells,
    proj,
    k1,
    k2,
    wb1,
    wb2,
    id_buf,
    id_recv,
    pcat,
    rows_out,
    rows_in,
    slot_row,
    sel,
    patch,
    partial,
    lhs_col,
    unperm,
    x1,
    x2,
    field,
    out,
    col_f,
    col_b,
    halo_b,
    halo_f,
    corner_out,
    corner_in,
    st_out,
    st_in,
    ld_sem,
    id_sem,
    row_sem,
    st_sem,
    halo_send,
    halo_recv,
    out_sem,
):
    g, i, j = (lax.axis_index(a) for a in AXES)
    me = g * 32 + i * 4 + j

    def dev(p):
        return (p // 32, (p // 4) % 8, p % 4)

    loads = [
        pltpu.make_async_copy(a, b, ld_sem.at[n])
        for n, (a, b) in enumerate(
            [(cells_hbm, cells), (proj_hbm, proj), (k1_hbm, k1), (k2_hbm, k2), (noisy_hbm, noisy)]
        )
    ]
    for c in loads:
        c.start()
    barrier = pltpu.get_barrier_semaphore()

    def greet(k, c):
        pl.semaphore_signal(barrier, inc=1, device_id=dev((me + k) % 128), device_id_type=MESH)
        return c

    lax.fori_loop(1, 128, greet, 0)

    def put_ids(o, c):
        id_buf[o, :, 0:MOST] = ids_ref[pl.ds(o, 1), :]
        return c

    lax.fori_loop(0, 128, put_ids, 0)
    id_recv[0, :, 0:MOST] = ids_ref[pl.ds(me, 1), :]
    pl.semaphore_wait(barrier, 127)

    def send_ids(k, c):
        p = (me + k) % 128
        pltpu.make_async_remote_copy(
            id_buf.at[p], id_recv.at[k], id_sem.at[0], id_sem.at[1], device_id=dev(p), device_id_type=MESH
        ).start()
        return c

    lax.fori_loop(1, 128, send_ids, 0)

    loads[0].wait()
    loads[1].wait()
    projected = jnp.dot(
        cells[...], proj[...], precision=lax.Precision.HIGHEST, preferred_element_type=F32
    )
    for n, term in enumerate(split3(projected)):
        pcat[:, n * 128 : (n + 1) * 128] = term
    rows_out[...] = jnp.zeros_like(rows_out)
    partial[...] = jnp.zeros_like(partial)

    slot_row[...] = jnp.full_like(slot_row, -1)
    slot_row[0:1, 0 : PATCH * PATCH] = slots_ref[...]
    slot = slot_row[0:1, :]
    owner = (slot * 10923) >> 16
    place = slot - owner * MOST
    index = ((owner - me + 128) & 127) * 8 + place
    index = jnp.where(slot < 0, -1, index).astype(F32)
    index = jnp.transpose(jnp.broadcast_to(index, (128, 256)))
    lane = lax.broadcasted_iota(jnp.int32, (256, 128), 1).astype(F32)
    for n in range(8):
        sel[:, n * 128 : (n + 1) * 128] = jnp.where(index == lane + 128.0 * n, 1.0, 0.0).astype(BF16)

    r_iota = lax.broadcasted_iota(jnp.int32, (128, 128), 0)
    l_iota = lax.broadcasted_iota(jnp.int32, (128, 128), 1)
    column = (r_iota % 16) * 8 + r_iota // 16
    lhs_col[:, 0:128] = weight_terms(column, l_iota, off_ref[0, 1]).astype(BF16)
    lhs_col[:, 128:256] = jnp.where(column == l_iota, 1.0, 0.0).astype(BF16)
    unperm[...] = jnp.where((l_iota % 16) * 8 + l_iota // 16 == r_iota, 1.0, 0.0).astype(BF16)
    lhs_row = weight_terms(r_iota, l_iota, off_ref[0, 0]).astype(BF16)

    loads[2].wait()
    loads[3].wait()
    zero_block = jnp.zeros((128, 128), BF16)
    for w, wb in ((k1, wb1), (k2, wb2)):
        for a in range(4):
            for b in range(3):
                for e in range(2):
                    block = w[a - e, b] if 0 <= a - e <= 2 else zero_block
                    wb[(a * 3 + b) * 128 : (a * 3 + b + 1) * 128, e * 128 : (e + 1) * 128] = block

    def whole(ref, sem):
        return pltpu.make_async_copy(ref, ref, sem)

    whole(id_recv.at[pl.ds(1, 127)], id_sem.at[1]).wait()
    asked = id_recv[:, 0, :] - me * HELD
    row_iota = lax.broadcasted_iota(jnp.int32, (128, HELD), 1)
    for m in range(MOST):
        hot = jnp.where(asked[:, m : m + 1] == row_iota, 1.0, 0.0).astype(BF16)
        found = jnp.dot(hot, pcat[...], preferred_element_type=F32)
        found = found[:, 0:128] + found[:, 128:256] + found[:, 256:384]
        rows_out[pl.ds(m, 128, stride=8), :] = found
    rows_in[0:8, :] = rows_out[0:8, :]

    def send_rows(k, c):
        part = pl.ds(pl.multiple_of(k * 8, 8), 8)
        pltpu.make_async_remote_copy(
            rows_out.at[part],
            rows_in.at[part],
            row_sem.at[0],
            row_sem.at[1],
            device_id=dev((me - k + 128) % 128),
            device_id_type=MESH,
        ).start()
        return c

    lax.fori_loop(1, 128, send_rows, 0)
    whole(id_buf.at[pl.ds(1, 127)], id_sem.at[0]).wait()
    loads[4].wait()
    whole(rows_in.at[pl.ds(8, 1016)], row_sem.at[1]).wait()

    terms = jnp.concatenate(split3(rows_in[...]), axis=1)
    cell = jnp.dot(sel[...], terms, preferred_element_type=F32)
    patch[...] = cell[:, 0:128] + cell[:, 128:256] + cell[:, 256:384]
    zero_tile = jnp.zeros((32, 128), BF16)

    def stack_terms(x):
        hi, mid, lo = split3(x)
        return jnp.concatenate([hi, mid, lo, hi, mid, hi, zero_tile], axis=0)

    for b in range(PATCH):
        rhs = stack_terms(patch[pl.ds(b, 16, stride=PATCH), :])
        partial[pl.ds(b, 128, stride=16), :] = jnp.dot(lhs_row, rhs, preferred_element_type=F32)

    def mix_pair(p):
        rhs = []
        for e in range(2):
            h = 2 * p + e
            t = stack_terms(partial[pl.ds(pl.multiple_of(h * 16, 16), 16), :])
            rhs.append(jnp.concatenate([t, noisy[h]], axis=0))
        mixed = jnp.dot(
            lhs_col[...], jnp.concatenate(rhs, axis=1), preferred_element_type=F32
        ).astype(BF16)
        for e in range(2):
            h = 2 * p + e
            m = mixed[:, e * 128 : (e + 1) * 128]
            x1[h + 1, 1:9] = m.reshape(8, 16, 128)
            mf = m.astype(F32)
            col_f[0, pl.ds(h, 1), :] = mf[0:1]
            col_f[1, pl.ds(h, 1), :] = mf[127:128]

    def neighbour(di, dj):
        return (g, (i + di + 8) % 8, (j + dj + 4) % 4)

    def row_copies(x, base):
        cs = []
        for n, (src, dst, di) in enumerate(((1, 129, -1), (128, 0, 1))):
            cs.append(
                pltpu.make_async_remote_copy(
                    x.at[src, pl.ds(1, 8)],
                    x.at[dst, pl.ds(1, 8)],
                    halo_send.at[base + n],
                    halo_recv.at[base + n],
                    device_id=neighbour(di, 0),
                    device_id_type=MESH,
                )
            )
        return cs

    def corner_copies(base):
        cs = []
        for n, (di, dj) in enumerate(((-1, -1), (-1, 1), (1, -1), (1, 1))):
            slot_n = base // 8 * 4 + n
            cs.append(
                pltpu.make_async_remote_copy(
                    corner_out.at[slot_n],
                    corner_in.at[slot_n],
                    halo_send.at[base + 4 + n],
                    halo_recv.at[base + 4 + n],
                    device_id=neighbour(di, dj),
                    device_id_type=MESH,
                )
            )
        return cs

    def col_copies(base):
        cs = []
        for n, dj in enumerate((-1, 1)):
            slot_n = base // 8 * 2 + n
            cs.append(
                pltpu.make_async_remote_copy(
                    col_b.at[slot_n],
                    halo_b.at[slot_n],
                    halo_send.at[base + 2 + n],
                    halo_recv.at[base + 2 + n],
                    device_id=neighbour(0, dj),
                    device_id_type=MESH,
                )
            )
        return cs

    def put_corners(base):
        s = base // 8 * 4
        for n, (side, h) in enumerate(((0, 0), (1, 0), (0, 127), (1, 127))):
            corner_out[s + n] = jnp.broadcast_to(col_f[side, h : h + 1, :], (8, 128))

    def put_columns(base):
        s = base // 8 * 2
        for side in range(2):
            col_b[s + side] = col_f[side].astype(BF16)

    def finish_halo(x, base, copies):
        for c in copies:
            c.wait()
        s2, s4 = base // 8 * 2, base // 8 * 4
        left_ok = jnp.where(j > 0, 1.0, 0.0)
        right_ok = jnp.where(j < 3, 1.0, 0.0)
        up_ok = jnp.where(i > 0, 1.0, 0.0)
        down_ok = jnp.where(i < 7, 1.0, 0.0)
        halo_f[0, 8:136, :] = halo_b[s2 + 1].astype(F32) * left_ok
        halo_f[1, 8:136, :] = halo_b[s2 + 0].astype(F32) * right_ok
        halo_f[0, 0:8, :] = corner_in[s4 + 3] * (left_ok * up_ok)
        halo_f[1, 0:8, :] = corner_in[s4 + 2] * (right_ok * up_ok)
        halo_f[0, 136:144, :] = corner_in[s4 + 1] * (left_ok * down_ok)
        halo_f[1, 136:144, :] = corner_in[s4 + 0] * (right_ok * down_ok)

        @pl.when(i == 0)
        def _():
            x[0, 1:9] = jnp.zeros((8, 16, 128), BF16)

        @pl.when(i == 7)
        def _():
            x[129, 1:9] = jnp.zeros((8, 16, 128), BF16)

        sub = lax.broadcasted_iota(jnp.int32, (16, 128), 0)

        def edge(n, c):
            last = pltpu.roll(x[n, 8].astype(F32), 1, 0)
            x[n, 0] = jnp.where(sub == 0, halo_f[0, pl.ds(n + 7, 1), :], last).astype(BF16)
            first = pltpu.roll(x[n, 1].astype(F32), 15, 0)
            x[n, 9] = jnp.where(sub == 15, halo_f[1, pl.ds(n + 7, 1), :], first).astype(BF16)
            return c

        lax.fori_loop(0, 130, edge, 0, unroll=5)

    mix_pair(0)
    mix_pair(63)
    halo1 = row_copies(x1, 0) + corner_copies(0)
    put_corners(0)
    for c in halo1:
        c.start()

    def mix_loop(p, c):
        mix_pair(p)
        return c

    lax.fori_loop(1, 63, mix_loop, 0, unroll=2)
    put_columns(0)
    cols1 = col_copies(0)
    for c in cols1:
        c.start()
    finish_halo(x1, 0, halo1 + cols1)

    def convolve(x, wb):
        def step(t, carry):
            total, square = carry
            y = t * (2 * PAIRS)
            lhs = []
            for q in range(PAIRS):
                parts = [
                    x[y + 2 * q + a, b : b + 8].reshape(128, 128) for a in range(4) for b in range(3)
                ]
                lhs.append(jnp.concatenate(parts, axis=1))
            got = jnp.dot(jnp.concatenate(lhs, axis=0), wb[...], preferred_element_type=F32)
            for q in range(PAIRS):
                for e in range(2):
                    v = got[q * 128 : (q + 1) * 128, e * 128 : (e + 1) * 128]
                    field[y + 2 * q + e] = v
                    v3 = v.reshape(16, 8, 128)
                    total = total + jnp.sum(v3, axis=0)
                    square = square + jnp.sum(v3 * v3, axis=0)
            return total, square

        zero = jnp.zeros((8, 128), F32)
        return lax.fori_loop(0, 64 // PAIRS, step, (zero, zero))

    group_ones = jnp.where(r_iota // 4 == l_iota // 4, 1.0, 0.0)
    number = float(TILE * TILE * 32 * (C // GROUPS))

    def norm_terms(n, sums, gain, shift):
        total, square = (jnp.sum(s, axis=0, keepdims=True) for s in sums)
        sub8 = lax.broadcasted_iota(jnp.int32, (8, 128), 0)
        mine = jnp.where(sub8 == 0, total, jnp.where(sub8 == 1, square, 0.0))
        st_out[n] = mine
        st_in[n, 0] = mine
        base = g * 32
        home = i * 4 + j

        def send(k, c):
            pltpu.make_async_remote_copy(
                st_out.at[n],
                st_in.at[n, k],
                st_sem.at[n, 0],
                st_sem.at[n, 1],
                device_id=dev(base + (home + k) % 32),
                device_id_type=MESH,
            ).start()
            return c

        lax.fori_loop(1, 32, send, 0)
        whole(st_in.at[n, pl.ds(1, 31)], st_sem.at[n, 1]).wait()
        both = jnp.sum(st_in[n], axis=0)
        both = jnp.dot(
            both, group_ones, precision=lax.Precision.HIGHEST, preferred_element_type=F32
        )
        mean = both[0:1] / number
        spread = both[1:2] / number - mean * mean
        scale = lax.rsqrt(spread + 1e-05) * gain
        whole(st_in.at[n, pl.ds(1, 31)], st_sem.at[n, 0]).wait()
        return scale, shift - mean * scale

    sums = convolve(x1, wb1)
    scale, offset = norm_terms(0, sums, g1_ref[...], s1_ref[...])

    def hide(h, lo, hi):
        v = field[h, lo * 16 : hi * 16, :]
        m = silu(v * scale + offset).astype(BF16)
        x2[h + 1, 1 + lo : 1 + hi] = m.reshape(hi - lo, 16, 128)
        return m.astype(F32)

    def hide_ends(h, c):
        a = hide(h, 0, 1)
        b = hide(h, 7, 8)
        col_f[0, pl.ds(h, 1), :] = a[0:1]
        col_f[1, pl.ds(h, 1), :] = b[15:16]
        return c

    def hide_rest(h, c):
        hide(h, 1, 7)
        return c

    for h in (0, 127):
        hide_ends(h, 0)
        hide_rest(h, 0)
    halo2 = row_copies(x2, 8) + corner_copies(8)
    put_corners(8)
    for c in halo2:
        c.start()
    lax.fori_loop(1, 127, hide_ends, 0, unroll=6)
    put_columns(8)
    cols2 = col_copies(8)
    for c in cols2:
        c.start()
    lax.fori_loop(1, 127, hide_rest, 0, unroll=2)
    finish_halo(x2, 8, halo2 + cols2)

    sums = convolve(x2, wb2)
    scale2, offset2 = norm_terms(1, sums, g2_ref[...], s2_ref[...])

    def finish(p, c):
        both = []
        for e in range(2):
            h = 2 * p + e
            v = silu(field[h] * scale2 + offset2)
            both.append((x1[h + 1, 1:9].reshape(128, 128).astype(F32) + v).astype(BF16))
        res = jnp.dot(unperm[...], jnp.concatenate(both, axis=1), preferred_element_type=F32).astype(BF16)
        out[2 * p] = res[:, 0:128]
        out[2 * p + 1] = res[:, 128:256]
        return c

    parts = 8
    for n in range(parts):
        lax.fori_loop(n * 64 // parts, (n + 1) * 64 // parts, finish, 0, unroll=2)
        rows = pl.ds(n * 128 // parts, 128 // parts)
        pltpu.make_async_copy(out.at[rows], out_hbm.at[rows], out_sem).start()
    whole(rows_in.at[pl.ds(8, 1016)], row_sem.at[0]).wait()
    pltpu.make_async_copy(out, out_hbm, out_sem).wait()


def body(
    noisy_field,
    coarse_cells,
    coarse_proj,
    kernel_first,
    kernel_second,
    gain_first,
    shift_first,
    gain_second,
    shift_second,
    request_ids,
    patch_slots,
    tile_offsets,
):
    hbm = pl.BlockSpec(memory_space=pl.ANY)
    vmem = pl.BlockSpec(memory_space=pltpu.VMEM)
    smem = pl.BlockSpec(memory_space=pltpu.SMEM)
    row = lambda v: v.reshape(1, C)
    got = pl.pallas_call(
        kernel,
        out_shape=jax.ShapeDtypeStruct((TILE, TILE, C), BF16),
        in_specs=[hbm] * 5 + [vmem] * 6 + [smem],
        out_specs=hbm,
        scratch_shapes=[
            pltpu.VMEM((TILE, TILE, C), BF16),
            pltpu.VMEM((HELD, CC), F32),
            pltpu.VMEM((CC, C), F32),
            pltpu.VMEM((3, 3, C, C), BF16),
            pltpu.VMEM((3, 3, C, C), BF16),
            pltpu.VMEM((12 * C, 2 * C), BF16),
            pltpu.VMEM((12 * C, 2 * C), BF16),
            pltpu.VMEM((128, 1, 128), jnp.int32),
            pltpu.VMEM((128, 1, 128), jnp.int32),
            pltpu.VMEM((HELD, 3 * C), BF16),
            pltpu.VMEM((1024, C), F32),
            pltpu.VMEM((1024, C), F32),
            pltpu.VMEM((8, 256), jnp.int32),
            pltpu.VMEM((256, 1024), BF16),
            pltpu.VMEM((256, C), F32),
            pltpu.VMEM((TILE * 16, C), F32),
            pltpu.VMEM((128, 256), BF16),
            pltpu.VMEM((128, 128), BF16),
            pltpu.VMEM((TILE + 2, 10, 16, C), BF16),
            pltpu.VMEM((TILE + 2, 10, 16, C), BF16),
            pltpu.VMEM((TILE, TILE, C), F32),
            pltpu.VMEM((TILE, TILE, C), BF16),
            pltpu.VMEM((2, TILE, C), F32),
            pltpu.VMEM((4, TILE, C), BF16),
            pltpu.VMEM((4, TILE, C), BF16),
            pltpu.VMEM((2, 144, C), F32),
            pltpu.VMEM((8, 8, C), F32),
            pltpu.VMEM((8, 8, C), F32),
            pltpu.VMEM((2, 8, C), F32),
            pltpu.VMEM((2, 32, 8, C), F32),
            pltpu.SemaphoreType.DMA((5,)),
            pltpu.SemaphoreType.DMA((2,)),
            pltpu.SemaphoreType.DMA((2,)),
            pltpu.SemaphoreType.DMA((2, 2)),
            pltpu.SemaphoreType.DMA((16,)),
            pltpu.SemaphoreType.DMA((16,)),
            pltpu.SemaphoreType.DMA,
        ],
        compiler_params=pltpu.CompilerParams(
            collective_id=0, has_side_effects=True, vmem_limit_bytes=60 << 20
        ),
        name="block",
    )(
        noisy_field.reshape(TILE, TILE, C),
        coarse_cells,
        coarse_proj,
        kernel_first,
        kernel_second,
        row(gain_first),
        row(shift_first),
        row(gain_second),
        row(shift_second),
        request_ids.reshape(128, MOST),
        patch_slots.reshape(1, PATCH * PATCH),
        tile_offsets.reshape(1, 2),
    )
    return got[None]


def solution(mesh):
    return jax.shard_map(
        body,
        mesh=mesh,
        in_specs=(
            P("region", "row", "col", None),
            P(("region", "row", "col"), None),
            P(),
            P(),
            P(),
            P(),
            P(),
            P(),
            P(),
            P("region", "row", "col", None, None),
            P("region", "row", "col", None),
            P("region", "row", "col", None),
        ),
        out_specs=P("region", "row", "col", None),
        check_vma=False,
    )
```

profile of v0, /device:TPU:1, one launch (start us, length us, event | category | flops | bytes accessed | tf_op | source)
XLA Modules:
  0.0 93.4 jit_solution(3188075260545311218)
XLA Ops:
  0.0 1.4 %copy.13 = s32[1,1,1,128,6]{4,3,2,1,0:T(8,128)} copy(s32[1,1,1,128,6]{3,2,4,1,0:T(1,128)} %param.21) | data formatting | bytes 6144 | tf_op args[9]
  1.4 87.2 %block.1 = bf16[128,128,128]{2,1,0:T(8,128)(2,1)} custom-call(bf16[128,128,128]{2,1,0:T(8,128)(2,1)} %bitcast.10, f32[256,640]{1,0:T(8,128)} %cells_hbm.1, f32[640,128]{1,0:T(8,128)} %proj_hbm.1, bf16[3,3,128,128]{3,2,1,0:T(8,128)(2,1)} %k1_hbm.1, bf16[3,3,128,128]{3,2,1,0:T(8,128)(2,1)} %k2_hbm.1, f32[1,128]{1,0:T(1,128)} %bitcast.13, f32[1,128]{1,0:T(1,128)} %bitcast.14, ...), custom_call_target="tpu_custom_call" | custom-call | tf_op jit(solution)/shard_map/block/pallas_call | solution.py:491
  88.6 4.8 %copy.15 = bf16[1,128,128,128]{3,2,1,0:T(8,128)(2,1)} copy(bf16[1,128,128,128]{3,2,1,0:T(8,128)(2,1)} %bitcast.9) | data formatting | bytes 8388608
where the time goes:
time: 93.6 us; the launch traced here: 93.4 us
  Pallas kernels  87.2 us (93%)
  local copies, waits for them, and re-layouts  6.21 us (7%)
    pallas_call x1, Pallas kernels, body(): pl.pallas_call(kernel, out_shape=jax.ShapeDtypeStruct((TILE, TILE, C), BF...  87.2 us
    unnamed x2, local copies, waits for them, and re-layouts  6.21 us

commit v1 on v0

--- a/solution.py
+++ b/solution.py
@@ -17,9 +17,10 @@
 HELD = 256
 AXES = ("region", "row", "col")
 MESH = pl.DeviceIdType.MESH
+FLAT = pl.DeviceIdType.LOGICAL
 F32 = jnp.float32
 BF16 = jnp.bfloat16
-PAIRS = 4
+PAIRS = 16
 
 
 def split3(x):
@@ -47,8 +48,11 @@
 
 
 def silu(v):
-    half = 0.5 * v
-    return half + half * jnp.tanh(half)
+    return v * jax.nn.sigmoid(v)
+
+
+def far_first(n):
+    return (~n & 0b1010100) | ((n ^ (n >> 1)) & 0b0101010) | (~n & 1)
 
 
 def kernel(
@@ -64,7 +68,7 @@
     ids_ref,
     slots_ref,
     off_ref,
-    out_hbm,
+    out,
     noisy,
     cells,
     proj,
@@ -72,6 +76,7 @@
     k2,
     wb1,
     wb2,
+    id_rows,
     id_buf,
     id_recv,
     pcat,
@@ -82,11 +87,10 @@
     patch,
     partial,
     lhs_col,
-    unperm,
     x1,
     x2,
     field,
-    out,
+    swap,
     col_f,
     col_b,
     halo_b,
@@ -101,13 +105,9 @@
     st_sem,
     halo_send,
     halo_recv,
-    out_sem,
 ):
     g, i, j = (lax.axis_index(a) for a in AXES)
     me = g * 32 + i * 4 + j
-
-    def dev(p):
-        return (p // 32, (p // 4) % 8, p % 4)
 
     loads = [
         pltpu.make_async_copy(a, b, ld_sem.at[n])
@@ -119,28 +119,26 @@
         c.start()
     barrier = pltpu.get_barrier_semaphore()
 
-    def greet(k, c):
-        pl.semaphore_signal(barrier, inc=1, device_id=dev((me + k) % 128), device_id_type=MESH)
-        return c
-
-    lax.fori_loop(1, 128, greet, 0)
-
-    def put_ids(o, c):
-        id_buf[o, :, 0:MOST] = ids_ref[pl.ds(o, 1), :]
-        return c
-
-    lax.fori_loop(0, 128, put_ids, 0)
-    id_recv[0, :, 0:MOST] = ids_ref[pl.ds(me, 1), :]
+    def greet(n, c):
+        pl.semaphore_signal(barrier, inc=1, device_id=me ^ far_first(n), device_id_type=FLAT)
+        return c
+
+    lax.fori_loop(0, 127, greet, 0)
+
+    id_rows[...] = jnp.zeros_like(id_rows)
+    id_rows[0:MOST, :] = ids_ref[...].astype(F32)
+    id_buf[:, 0, :] = jnp.transpose(id_rows[...])
+    id_recv[0] = id_buf[me]
     pl.semaphore_wait(barrier, 127)
 
-    def send_ids(k, c):
-        p = (me + k) % 128
+    def send_ids(n, c):
+        k = far_first(n)
         pltpu.make_async_remote_copy(
-            id_buf.at[p], id_recv.at[k], id_sem.at[0], id_sem.at[1], device_id=dev(p), device_id_type=MESH
+            id_buf.at[me ^ k], id_recv.at[k], id_sem.at[0], id_sem.at[1], device_id=me ^ k, device_id_type=FLAT
         ).start()
         return c
 
-    lax.fori_loop(1, 128, send_ids, 0)
+    lax.fori_loop(0, 127, send_ids, 0)
 
     loads[0].wait()
     loads[1].wait()
@@ -149,7 +147,6 @@
     )
     for n, term in enumerate(split3(projected)):
         pcat[:, n * 128 : (n + 1) * 128] = term
-    rows_out[...] = jnp.zeros_like(rows_out)
     partial[...] = jnp.zeros_like(partial)
 
     slot_row[...] = jnp.full_like(slot_row, -1)
@@ -157,11 +154,11 @@
     slot = slot_row[0:1, :]
     owner = (slot * 10923) >> 16
     place = slot - owner * MOST
-    index = ((owner - me + 128) & 127) * 8 + place
+    index = place * 128 + (owner ^ me)
     index = jnp.where(slot < 0, -1, index).astype(F32)
     index = jnp.transpose(jnp.broadcast_to(index, (128, 256)))
     lane = lax.broadcasted_iota(jnp.int32, (256, 128), 1).astype(F32)
-    for n in range(8):
+    for n in range(MOST):
         sel[:, n * 128 : (n + 1) * 128] = jnp.where(index == lane + 128.0 * n, 1.0, 0.0).astype(BF16)
 
     r_iota = lax.broadcasted_iota(jnp.int32, (128, 128), 0)
@@ -169,7 +166,6 @@
     column = (r_iota % 16) * 8 + r_iota // 16
     lhs_col[:, 0:128] = weight_terms(column, l_iota, off_ref[0, 1]).astype(BF16)
     lhs_col[:, 128:256] = jnp.where(column == l_iota, 1.0, 0.0).astype(BF16)
-    unperm[...] = jnp.where((l_iota % 16) * 8 + l_iota // 16 == r_iota, 1.0, 0.0).astype(BF16)
     lhs_row = weight_terms(r_iota, l_iota, off_ref[0, 0]).astype(BF16)
 
     loads[2].wait()
@@ -186,34 +182,34 @@
         return pltpu.make_async_copy(ref, ref, sem)
 
     whole(id_recv.at[pl.ds(1, 127)], id_sem.at[1]).wait()
-    asked = id_recv[:, 0, :] - me * HELD
-    row_iota = lax.broadcasted_iota(jnp.int32, (128, HELD), 1)
+    asked = id_recv[:, 0, :] - (me * HELD).astype(F32)
+    row_iota = lax.broadcasted_iota(jnp.int32, (128, HELD), 1).astype(F32)
     for m in range(MOST):
         hot = jnp.where(asked[:, m : m + 1] == row_iota, 1.0, 0.0).astype(BF16)
         found = jnp.dot(hot, pcat[...], preferred_element_type=F32)
         found = found[:, 0:128] + found[:, 128:256] + found[:, 256:384]
-        rows_out[pl.ds(m, 128, stride=8), :] = found
-    rows_in[0:8, :] = rows_out[0:8, :]
-
-    def send_rows(k, c):
-        part = pl.ds(pl.multiple_of(k * 8, 8), 8)
+        rows_out[:, m, :] = found
+    rows_in[0] = rows_out[0]
+
+    def send_rows(n, c):
+        k = far_first(n)
         pltpu.make_async_remote_copy(
-            rows_out.at[part],
-            rows_in.at[part],
+            rows_out.at[k],
+            rows_in.at[k],
             row_sem.at[0],
             row_sem.at[1],
-            device_id=dev((me - k + 128) % 128),
-            device_id_type=MESH,
+            device_id=me ^ k,
+            device_id_type=FLAT,
         ).start()
         return c
 
-    lax.fori_loop(1, 128, send_rows, 0)
+    lax.fori_loop(0, 127, send_rows, 0)
     whole(id_buf.at[pl.ds(1, 127)], id_sem.at[0]).wait()
     loads[4].wait()
-    whole(rows_in.at[pl.ds(8, 1016)], row_sem.at[1]).wait()
-
-    terms = jnp.concatenate(split3(rows_in[...]), axis=1)
-    cell = jnp.dot(sel[...], terms, preferred_element_type=F32)
+    whole(rows_in.at[pl.ds(1, 127)], row_sem.at[1]).wait()
+
+    terms = [jnp.concatenate(split3(rows_in[:, m, :]), axis=1) for m in range(MOST)]
+    cell = jnp.dot(sel[...], jnp.concatenate(terms, axis=0), preferred_element_type=F32)
     patch[...] = cell[:, 0:128] + cell[:, 128:256] + cell[:, 256:384]
     zero_tile = jnp.zeros((32, 128), BF16)
 
@@ -225,22 +221,21 @@
         rhs = stack_terms(patch[pl.ds(b, 16, stride=PATCH), :])
         partial[pl.ds(b, 128, stride=16), :] = jnp.dot(lhs_row, rhs, preferred_element_type=F32)
 
-    def mix_pair(p):
+    def mix_rows(first, count):
         rhs = []
-        for e in range(2):
-            h = 2 * p + e
+        for q in range(count):
+            h = first + q
             t = stack_terms(partial[pl.ds(pl.multiple_of(h * 16, 16), 16), :])
             rhs.append(jnp.concatenate([t, noisy[h]], axis=0))
         mixed = jnp.dot(
             lhs_col[...], jnp.concatenate(rhs, axis=1), preferred_element_type=F32
         ).astype(BF16)
-        for e in range(2):
-            h = 2 * p + e
-            m = mixed[:, e * 128 : (e + 1) * 128]
+        for q in range(count):
+            h = first + q
+            m = mixed[:, q * 128 : (q + 1) * 128]
             x1[h + 1, 1:9] = m.reshape(8, 16, 128)
-            mf = m.astype(F32)
-            col_f[0, pl.ds(h, 1), :] = mf[0:1]
-            col_f[1, pl.ds(h, 1), :] = mf[127:128]
+            col_f[0, pl.ds(h, 1), :] = m[0:16].astype(F32)[0:1]
+            col_f[1, pl.ds(h, 1), :] = m[112:128].astype(F32)[15:16]
 
     def neighbour(di, dj):
         return (g, (i + di + 8) % 8, (j + dj + 4) % 4)
@@ -302,16 +297,35 @@
         for side in range(2):
             col_b[s + side] = col_f[side].astype(BF16)
 
-    def finish_halo(x, base, copies):
+    left_ok = jnp.where(j > 0, 1.0, 0.0)
+    right_ok = jnp.where(j < 3, 1.0, 0.0)
+    up_ok = jnp.where(i > 0, 1.0, 0.0)
+    down_ok = jnp.where(i < 7, 1.0, 0.0)
+    sub = lax.broadcasted_iota(jnp.int32, (16, 128), 0)
+
+    def edge(x, n):
+        last = pltpu.roll(x[n, 8].astype(F32), 1, 0)
+        x[n, 0] = jnp.where(sub == 0, halo_f[0, pl.ds(n + 7, 1), :], last).astype(BF16)
+        first = pltpu.roll(x[n, 1].astype(F32), 15, 0)
+        x[n, 9] = jnp.where(sub == 15, halo_f[1, pl.ds(n + 7, 1), :], first).astype(BF16)
+
+    def finish_columns(x, base, copies):
         for c in copies:
             c.wait()
-        s2, s4 = base // 8 * 2, base // 8 * 4
-        left_ok = jnp.where(j > 0, 1.0, 0.0)
-        right_ok = jnp.where(j < 3, 1.0, 0.0)
-        up_ok = jnp.where(i > 0, 1.0, 0.0)
-        down_ok = jnp.where(i < 7, 1.0, 0.0)
+        s2 = base // 8 * 2
         halo_f[0, 8:136, :] = halo_b[s2 + 1].astype(F32) * left_ok
         halo_f[1, 8:136, :] = halo_b[s2 + 0].astype(F32) * right_ok
+
+        def step(n, c):
+            edge(x, n)
+            return c
+
+        lax.fori_loop(1, 129, step, 0, unroll=8)
+
+    def finish_rows(x, base, copies):
+        for c in copies:
+            c.wait()
+        s4 = base // 8 * 4
         halo_f[0, 0:8, :] = corner_in[s4 + 3] * (left_ok * up_ok)
         halo_f[1, 0:8, :] = corner_in[s4 + 2] * (right_ok * up_ok)
         halo_f[0, 136:144, :] = corner_in[s4 + 1] * (left_ok * down_ok)
@@ -325,36 +339,28 @@
         def _():
             x[129, 1:9] = jnp.zeros((8, 16, 128), BF16)
 
-        sub = lax.broadcasted_iota(jnp.int32, (16, 128), 0)
-
-        def edge(n, c):
-            last = pltpu.roll(x[n, 8].astype(F32), 1, 0)
-            x[n, 0] = jnp.where(sub == 0, halo_f[0, pl.ds(n + 7, 1), :], last).astype(BF16)
-            first = pltpu.roll(x[n, 1].astype(F32), 15, 0)
-            x[n, 9] = jnp.where(sub == 15, halo_f[1, pl.ds(n + 7, 1), :], first).astype(BF16)
-            return c
-
-        lax.fori_loop(0, 130, edge, 0, unroll=5)
-
-    mix_pair(0)
-    mix_pair(63)
+        edge(x, 0)
+        edge(x, 129)
+
+    mix_rows(0, 2)
+    mix_rows(126, 2)
     halo1 = row_copies(x1, 0) + corner_copies(0)
     put_corners(0)
     for c in halo1:
         c.start()
 
-    def mix_loop(p, c):
-        mix_pair(p)
-        return c
-
-    lax.fori_loop(1, 63, mix_loop, 0, unroll=2)
+    def mix_loop(n, c):
+        mix_rows(2 + n * 32, 32)
+        return c
+
+    lax.fori_loop(0, 3, mix_loop, 0)
+    mix_rows(98, 28)
     put_columns(0)
     cols1 = col_copies(0)
     for c in cols1:
         c.start()
-    finish_halo(x1, 0, halo1 + cols1)
-
-    def convolve(x, wb):
+
+    def convolve(x, wb, base, columns, rows):
         def step(t, carry):
             total, square = carry
             y = t * (2 * PAIRS)
@@ -374,8 +380,12 @@
                     square = square + jnp.sum(v3 * v3, axis=0)
             return total, square
 
+        blocks = 64 // PAIRS
         zero = jnp.zeros((8, 128), F32)
-        return lax.fori_loop(0, 64 // PAIRS, step, (zero, zero))
+        finish_columns(x, base, columns)
+        sums = lax.fori_loop(1, blocks - 1, step, (zero, zero))
+        finish_rows(x, base, rows)
+        return lax.fori_loop(0, 2, lambda n, c: step(n * (blocks - 1), c), sums)
 
     group_ones = jnp.where(r_iota // 4 == l_iota // 4, 1.0, 0.0)
     number = float(TILE * TILE * 32 * (C // GROUPS))
@@ -386,21 +396,19 @@
         mine = jnp.where(sub8 == 0, total, jnp.where(sub8 == 1, square, 0.0))
         st_out[n] = mine
         st_in[n, 0] = mine
-        base = g * 32
-        home = i * 4 + j
-
-        def send(k, c):
+        def send(t, c):
+            k = far_first(t)
             pltpu.make_async_remote_copy(
                 st_out.at[n],
                 st_in.at[n, k],
                 st_sem.at[n, 0],
                 st_sem.at[n, 1],
-                device_id=dev(base + (home + k) % 32),
-                device_id_type=MESH,
+                device_id=me ^ k,
+                device_id_type=FLAT,
             ).start()
             return c
 
-        lax.fori_loop(1, 32, send, 0)
+        lax.fori_loop(96, 127, send, 0)
         whole(st_in.at[n, pl.ds(1, 31)], st_sem.at[n, 1]).wait()
         both = jnp.sum(st_in[n], axis=0)
         both = jnp.dot(
@@ -412,7 +420,7 @@
         whole(st_in.at[n, pl.ds(1, 31)], st_sem.at[n, 0]).wait()
         return scale, shift - mean * scale
 
-    sums = convolve(x1, wb1)
+    sums = convolve(x1, wb1, 0, cols1, halo1)
     scale, offset = norm_terms(0, sums, g1_ref[...], s1_ref[...])
 
     def hide(h, lo, hi):
@@ -432,42 +440,35 @@
         hide(h, 1, 7)
         return c
 
-    for h in (0, 127):
-        hide_ends(h, 0)
-        hide_rest(h, 0)
+    lax.fori_loop(0, 128, hide_ends, 0, unroll=8)
+    put_columns(8)
+    cols2 = col_copies(8)
+    for c in cols2:
+        c.start()
+    hide_rest(0, 0)
+    hide_rest(127, 0)
     halo2 = row_copies(x2, 8) + corner_copies(8)
     put_corners(8)
     for c in halo2:
         c.start()
-    lax.fori_loop(1, 127, hide_ends, 0, unroll=6)
-    put_columns(8)
-    cols2 = col_copies(8)
-    for c in cols2:
-        c.start()
-    lax.fori_loop(1, 127, hide_rest, 0, unroll=2)
-    finish_halo(x2, 8, halo2 + cols2)
-
-    sums = convolve(x2, wb2)
+    lax.fori_loop(1, 127, hide_rest, 0, unroll=7)
+
+    sums = convolve(x2, wb2, 8, cols2, halo2)
     scale2, offset2 = norm_terms(1, sums, g2_ref[...], s2_ref[...])
 
-    def finish(p, c):
-        both = []
-        for e in range(2):
-            h = 2 * p + e
+    def finish(n, c):
+        for q in range(8):
+            h = n * 8 + q
             v = silu(field[h] * scale2 + offset2)
-            both.append((x1[h + 1, 1:9].reshape(128, 128).astype(F32) + v).astype(BF16))
-        res = jnp.dot(unperm[...], jnp.concatenate(both, axis=1), preferred_element_type=F32).astype(BF16)
-        out[2 * p] = res[:, 0:128]
-        out[2 * p + 1] = res[:, 128:256]
-        return c
-
-    parts = 8
-    for n in range(parts):
-        lax.fori_loop(n * 64 // parts, (n + 1) * 64 // parts, finish, 0, unroll=2)
-        rows = pl.ds(n * 128 // parts, 128 // parts)
-        pltpu.make_async_copy(out.at[rows], out_hbm.at[rows], out_sem).start()
-    whole(rows_in.at[pl.ds(8, 1016)], row_sem.at[0]).wait()
-    pltpu.make_async_copy(out, out_hbm, out_sem).wait()
+            v = x1[h + 1, 1:9].reshape(128, 128).astype(F32) + v
+            for s in range(8):
+                swap[q, pl.ds(s, 16, stride=8), :] = v[s * 16 : (s + 1) * 16]
+        for q in range(8):
+            out[n * 8 + q] = swap[q].astype(BF16)
+        return c
+
+    lax.fori_loop(0, 16, finish, 0)
+    whole(rows_in.at[pl.ds(1, 127)], row_sem.at[0]).wait()
 
 
 def body(
@@ -490,9 +491,9 @@
     row = lambda v: v.reshape(1, C)
     got = pl.pallas_call(
         kernel,
-        out_shape=jax.ShapeDtypeStruct((TILE, TILE, C), BF16),
+        out_shape=pltpu.VMEM((TILE, TILE, C), BF16),
         in_specs=[hbm] * 5 + [vmem] * 6 + [smem],
-        out_specs=hbm,
+        out_specs=vmem,
         scratch_shapes=[
             pltpu.VMEM((TILE, TILE, C), BF16),
             pltpu.VMEM((HELD, CC), F32),
@@ -501,21 +502,21 @@
             pltpu.VMEM((3, 3, C, C), BF16),
             pltpu.VMEM((12 * C, 2 * C), BF16),
             pltpu.VMEM((12 * C, 2 * C), BF16),
-            pltpu.VMEM((128, 1, 128), jnp.int32),
-            pltpu.VMEM((128, 1, 128), jnp.int32),
+            pltpu.VMEM((128, 128), F32),
+            pltpu.VMEM((128, 1, 128), F32),
+            pltpu.VMEM((128, 1, 128), F32),
             pltpu.VMEM((HELD, 3 * C), BF16),
-            pltpu.VMEM((1024, C), F32),
-            pltpu.VMEM((1024, C), F32),
+            pltpu.VMEM((128, MOST, C), F32),
+            pltpu.VMEM((128, MOST, C), F32),
             pltpu.VMEM((8, 256), jnp.int32),
-            pltpu.VMEM((256, 1024), BF16),
+            pltpu.VMEM((256, MOST * 128), BF16),
             pltpu.VMEM((256, C), F32),
             pltpu.VMEM((TILE * 16, C), F32),
             pltpu.VMEM((128, 256), BF16),
-            pltpu.VMEM((128, 128), BF16),
             pltpu.VMEM((TILE + 2, 10, 16, C), BF16),
             pltpu.VMEM((TILE + 2, 10, 16, C), BF16),
             pltpu.VMEM((TILE, TILE, C), F32),
-            pltpu.VMEM((TILE, TILE, C), BF16),
+            pltpu.VMEM((8, TILE, C), F32),
             pltpu.VMEM((2, TILE, C), F32),
             pltpu.VMEM((4, TILE, C), BF16),
             pltpu.VMEM((4, TILE, C), BF16),
@@ -530,10 +531,9 @@
             pltpu.SemaphoreType.DMA((2, 2)),
             pltpu.SemaphoreType.DMA((16,)),
             pltpu.SemaphoreType.DMA((16,)),
-            pltpu.SemaphoreType.DMA,
         ],
         compiler_params=pltpu.CompilerParams(
-            collective_id=0, has_side_effects=True, vmem_limit_bytes=60 << 20
+            collective_id=0, has_side_effects=True, vmem_limit_bytes=59 << 20
         ),
         name="block",
     )(
@@ -546,7 +546,7 @@
         row(shift_first),
         row(gain_second),
         row(shift_second),
-        request_ids.reshape(128, MOST),
+        request_ids.reshape(128, MOST).T,
         patch_slots.reshape(1, PATCH * PATCH),
         tile_offsets.reshape(1, 2),
     )

time: 93.6 us -> 68.4 us (0.73)
  Pallas kernels: 87.2 us -> 64.9 us
  local copies, waits for them, and re-layouts: 6.21 us -> 3.29 us
    pallas_call x1, Pallas kernels: 87.2 us -> 64.9 us  [body(): pl.pallas_call(kernel, out_shape=pltpu.VMEM((TILE, TILE, C), BF16), in_sp...]
    unnamed x2, local copies, waits for them, and re-layouts: 6.21 us -> 3.29 us
where the time goes in v1:
time: 68.4 us; the launch traced here: 68.2 us
  Pallas kernels  64.9 us (95%)
  local copies, waits for them, and re-layouts  3.29 us (5%)
    pallas_call x1, Pallas kernels, body(): pl.pallas_call(kernel, out_shape=pltpu.VMEM((TILE, TILE, C), BF16), in_sp...  64.9 us
    unnamed x2, local copies, waits for them, and re-layouts  3.29 us

profile of v1, /device:TPU:1, one launch (start us, length us, event | category | flops | bytes accessed | tf_op | source)
XLA Modules:
  0.0 68.2 jit_solution(1883421961384534051)
XLA Ops:
  0.0 1.3 %copy.15 = s32[1,1,1,128,6]{3,4,2,1,0:T(8,128)} copy(s32[1,1,1,128,6]{3,2,4,1,0:T(1,128)} %param.21) | data formatting | bytes 6144
  1.3 64.9 %block.1 = bf16[128,128,128]{2,1,0:T(8,128)(2,1)S(1)} custom-call(bf16[128,128,128]{2,1,0:T(8,128)(2,1)} %bitcast.14, f32[256,640]{1,0:T(8,128)} %cells_hbm.1, f32[640,128]{1,0:T(8,128)} %proj_hbm.1, bf16[3,3,128,128]{3,2,1,0:T(8,128)(2,1)} %k1_hbm.1, bf16[3,3,128,128]{3,2,1,0:T(8,128)(2,1)} %k2_hbm.1, f32[1,128]{1,0:T(1,128)} %bitcast.17, ...), custom_call_target="tpu_custom_call" | custom-call | tf_op jit(solution)/shard_map/block/pallas_call | solution.py:492
  66.2 2.0 %copy.17 = bf16[1,128,128,128]{3,2,1,0:T(8,128)(2,1)} copy(bf16[1,128,128,128]{3,2,1,0:T(8,128)(2,1)S(1)} %bitcast.13) | data formatting | bytes 8388608

commit v2 on v1

--- a/solution.py
+++ b/solution.py
@@ -45,6 +45,18 @@
     weight = jnp.where(cell < PATCH, weight, 0.0)
     hi, mid, lo = (t.astype(F32) for t in split3(weight))
     return jnp.where(group < 3, hi, jnp.where(group < 5, mid, jnp.where(group < 6, lo, 0.0)))
+
+
+def tap_terms(point, lane, offset):
+    group = (lane * 1366) >> 16
+    rest = lane - group * 48
+    point = point + (rest >> 4) - 1
+    cell = rest & 15
+    position = (offset.astype(F32) + point.astype(F32) * STEP) / 128.0 + 1.0
+    weight = cubic(jnp.abs(position - cell.astype(F32)))
+    weight = jnp.where((cell < PATCH) & (point >= 0) & (point < TILE), weight, 0.0)
+    hi, mid, _ = (t.astype(F32) for t in split3(weight))
+    return jnp.where(group < 2, hi, jnp.where(group < 3, mid, 0.0))
 
 
 def silu(v):
@@ -86,8 +98,16 @@
     sel,
     patch,
     partial,
+    row_out,
+    taps,
     lhs_col,
-    x1,
+    lhs_tap_row,
+    lhs_tap_col,
+    edge_sel,
+    noisy_col,
+    wtap,
+    rows_halo,
+    mixed,
     x2,
     field,
     swap,
@@ -126,7 +146,7 @@
     lax.fori_loop(0, 127, greet, 0)
 
     id_rows[...] = jnp.zeros_like(id_rows)
-    id_rows[0:MOST, :] = ids_ref[...].astype(F32)
+    id_rows[0:MOST, :] = ids_ref[:, 0, :].astype(F32)
     id_buf[:, 0, :] = jnp.transpose(id_rows[...])
     id_recv[0] = id_buf[me]
     pl.semaphore_wait(barrier, 127)
@@ -148,6 +168,7 @@
     for n, term in enumerate(split3(projected)):
         pcat[:, n * 128 : (n + 1) * 128] = term
     partial[...] = jnp.zeros_like(partial)
+    taps[...] = jnp.zeros_like(taps)
 
     slot_row[...] = jnp.full_like(slot_row, -1)
     slot_row[0:1, 0 : PATCH * PATCH] = slots_ref[...]
@@ -167,6 +188,21 @@
     lhs_col[:, 0:128] = weight_terms(column, l_iota, off_ref[0, 1]).astype(BF16)
     lhs_col[:, 128:256] = jnp.where(column == l_iota, 1.0, 0.0).astype(BF16)
     lhs_row = weight_terms(r_iota, l_iota, off_ref[0, 0]).astype(BF16)
+    r_tap = lax.broadcasted_iota(jnp.int32, (128, 144), 0)
+    l_tap = lax.broadcasted_iota(jnp.int32, (128, 144), 1)
+    lhs_tap_row[...] = tap_terms(r_tap, l_tap, off_ref[0, 0]).astype(BF16)
+    lhs_tap_col[...] = tap_terms((r_tap % 16) * 8 + r_tap // 16, l_tap, off_ref[0, 1]).astype(BF16)
+    e_row = lax.broadcasted_iota(jnp.int32, (64, 256), 0)
+    p_cell = lax.broadcasted_iota(jnp.int32, (64, 256), 1)
+    p_row = (p_cell * 5042) >> 16
+    p_col = p_cell - p_row * PATCH
+    on_rows = e_row < 32
+    point = jnp.where((e_row & 16) == 0, 0, TILE - 1)
+    start = jnp.where(on_rows, off_ref[0, 0], off_ref[0, 1])
+    position = (start.astype(F32) + point.astype(F32) * STEP) / 128.0 + 1.0
+    weight = cubic(jnp.abs(position - jnp.where(on_rows, p_row, p_col).astype(F32)))
+    keep = (jnp.where(on_rows, p_col, p_row) == (e_row & 15)) & (p_cell < PATCH * PATCH)
+    edge_sel[...] = jnp.where(keep, weight, 0.0)
 
     loads[2].wait()
     loads[3].wait()
@@ -177,6 +213,57 @@
                 for e in range(2):
                     block = w[a - e, b] if 0 <= a - e <= 2 else zero_block
                     wb[(a * 3 + b) * 128 : (a * 3 + b + 1) * 128, e * 128 : (e + 1) * 128] = block
+
+    for a in range(3):
+        for b in range(3):
+            n = a * 3 + b
+            wtap[0:128, n * 128 : (n + 1) * 128] = k1[a, b]
+            wtap[128:256, n * 128 : (n + 1) * 128] = k1[a, b]
+
+    sub = lax.broadcasted_iota(jnp.int32, (16, 128), 0)
+    x2[0] = jnp.zeros((160, 128), BF16)
+    x2[TILE + 1] = jnp.zeros((160, 128), BF16)
+    loads[4].wait()
+
+    def reorder(n, c):
+        h0 = n * 16
+        got = jnp.dot(
+            lhs_col[:, 128:256],
+            jnp.concatenate([noisy[h0 + q] for q in range(16)], axis=1),
+            preferred_element_type=F32,
+        )
+        for q in range(16):
+            v = got[:, q * 128 : (q + 1) * 128]
+            h = h0 + q
+            x2[h + 1, 16:144] = v.astype(BF16)
+            x2[h + 1, 0:16] = jnp.where(sub == 0, 0.0, pltpu.roll(v[112:128], 1, 0)).astype(BF16)
+            x2[h + 1, 144:160] = jnp.where(sub == 15, 0.0, pltpu.roll(v[0:16], 15, 0)).astype(BF16)
+            noisy_col[0, pl.ds(h, 1), :] = v[0:1]
+            noisy_col[1, pl.ds(h, 1), :] = v[127:128]
+        return c
+
+    lax.fori_loop(0, 8, reorder, 0)
+
+    def conv_block(x, wb, t):
+        y = t * (2 * PAIRS)
+        lhs = []
+        for q in range(PAIRS):
+            parts = [
+                x[y + 2 * q + a, b * 16 : b * 16 + 128] for a in range(4) for b in range(3)
+            ]
+            lhs.append(jnp.concatenate(parts, axis=1))
+        got = jnp.dot(jnp.concatenate(lhs, axis=0), wb[...], preferred_element_type=F32)
+        for q in range(PAIRS):
+            for e in range(2):
+                yield y + 2 * q + e, got[q * 128 : (q + 1) * 128, e * 128 : (e + 1) * 128]
+
+    def at_row(h):
+        return pl.ds(pl.multiple_of(h * 128, 128), 128)
+
+    def conv_noisy(t, c):
+        for h, v in conv_block(x2, wb1, t):
+            field[at_row(h), :] = v
+        return c
 
     def whole(ref, sem):
         return pltpu.make_async_copy(ref, ref, sem)
@@ -204,56 +291,69 @@
         return c
 
     lax.fori_loop(0, 127, send_rows, 0)
+    lax.fori_loop(0, 64 // PAIRS, conv_noisy, 0)
     whole(id_buf.at[pl.ds(1, 127)], id_sem.at[0]).wait()
-    loads[4].wait()
     whole(rows_in.at[pl.ds(1, 127)], row_sem.at[1]).wait()
 
     terms = [jnp.concatenate(split3(rows_in[:, m, :]), axis=1) for m in range(MOST)]
     cell = jnp.dot(sel[...], jnp.concatenate(terms, axis=0), preferred_element_type=F32)
-    patch[...] = cell[:, 0:128] + cell[:, 128:256] + cell[:, 256:384]
+    cell = cell[:, 0:128] + cell[:, 128:256] + cell[:, 256:384]
+    patch[9] = cell
     zero_tile = jnp.zeros((32, 128), BF16)
 
     def stack_terms(x):
         hi, mid, lo = split3(x)
         return jnp.concatenate([hi, mid, lo, hi, mid, hi, zero_tile], axis=0)
 
-    for b in range(PATCH):
-        rhs = stack_terms(patch[pl.ds(b, 16, stride=PATCH), :])
-        partial[pl.ds(b, 128, stride=16), :] = jnp.dot(lhs_row, rhs, preferred_element_type=F32)
-
-    def mix_rows(first, count):
-        rhs = []
-        for q in range(count):
-            h = first + q
-            t = stack_terms(partial[pl.ds(pl.multiple_of(h * 16, 16), 16), :])
-            rhs.append(jnp.concatenate([t, noisy[h]], axis=0))
-        mixed = jnp.dot(
-            lhs_col[...], jnp.concatenate(rhs, axis=1), preferred_element_type=F32
-        ).astype(BF16)
-        for q in range(count):
-            h = first + q
-            m = mixed[:, q * 128 : (q + 1) * 128]
-            x1[h + 1, 1:9] = m.reshape(8, 16, 128)
-            col_f[0, pl.ds(h, 1), :] = m[0:16].astype(F32)[0:1]
-            col_f[1, pl.ds(h, 1), :] = m[112:128].astype(F32)[15:16]
+    ends = jnp.dot(
+        edge_sel[...], cell, precision=lax.Precision.HIGHEST, preferred_element_type=F32
+    )
+    for side in range(2):
+        h = side * (TILE - 1)
+        rhs = jnp.concatenate([stack_terms(ends[side * 16 : side * 16 + 16]), noisy[h]], axis=0)
+        row_out[side] = jnp.dot(lhs_col[...], rhs, preferred_element_type=F32).astype(BF16)
+        rhs = stack_terms(ends[32 + side * 16 : 48 + side * 16])
+        got = noisy_col[side] + jnp.dot(lhs_row, rhs, preferred_element_type=F32)
+        col_b[side] = got.astype(BF16)
+        col_f[side] = col_b[side].astype(F32)
+
+    def form_mixed():
+        for b in range(PATCH):
+            rhs = stack_terms(patch[9, pl.ds(b, 16, stride=PATCH), :])
+            partial[pl.ds(b, 128, stride=16), :] = jnp.dot(
+                lhs_row, rhs, preferred_element_type=F32
+            )
+
+        def step(n, c):
+            rhs = []
+            for q in range(16):
+                h = n * 16 + q
+                t = stack_terms(partial[pl.ds(pl.multiple_of(h * 16, 16), 16), :])
+                rhs.append(jnp.concatenate([t, noisy[h]], axis=0))
+            got = jnp.dot(
+                lhs_col[...], jnp.concatenate(rhs, axis=1), preferred_element_type=F32
+            ).astype(BF16)
+            for q in range(16):
+                mixed[n * 16 + q] = got[:, q * 128 : (q + 1) * 128]
+            return c
+
+        lax.fori_loop(0, 8, step, 0)
 
     def neighbour(di, dj):
         return (g, (i + di + 8) % 8, (j + dj + 4) % 4)
 
-    def row_copies(x, base):
-        cs = []
-        for n, (src, dst, di) in enumerate(((1, 129, -1), (128, 0, 1))):
-            cs.append(
-                pltpu.make_async_remote_copy(
-                    x.at[src, pl.ds(1, 8)],
-                    x.at[dst, pl.ds(1, 8)],
-                    halo_send.at[base + n],
-                    halo_recv.at[base + n],
-                    device_id=neighbour(di, 0),
-                    device_id_type=MESH,
-                )
+    def row_copies(pairs, base):
+        return [
+            pltpu.make_async_remote_copy(
+                src,
+                dst,
+                halo_send.at[base + n],
+                halo_recv.at[base + n],
+                device_id=neighbour(di, 0),
+                device_id_type=MESH,
             )
-        return cs
+            for n, ((src, dst), di) in enumerate(zip(pairs, (-1, 1)))
+        ]
 
     def corner_copies(base):
         cs = []
@@ -301,96 +401,146 @@
     right_ok = jnp.where(j < 3, 1.0, 0.0)
     up_ok = jnp.where(i > 0, 1.0, 0.0)
     down_ok = jnp.where(i < 7, 1.0, 0.0)
-    sub = lax.broadcasted_iota(jnp.int32, (16, 128), 0)
 
     def edge(x, n):
-        last = pltpu.roll(x[n, 8].astype(F32), 1, 0)
-        x[n, 0] = jnp.where(sub == 0, halo_f[0, pl.ds(n + 7, 1), :], last).astype(BF16)
-        first = pltpu.roll(x[n, 1].astype(F32), 15, 0)
-        x[n, 9] = jnp.where(sub == 15, halo_f[1, pl.ds(n + 7, 1), :], first).astype(BF16)
-
-    def finish_columns(x, base, copies):
+        last = pltpu.roll(x[n, 128:144].astype(F32), 1, 0)
+        x[n, 0:16] = jnp.where(sub == 0, halo_f[0, pl.ds(n + 7, 1), :], last).astype(BF16)
+        first = pltpu.roll(x[n, 16:32].astype(F32), 15, 0)
+        x[n, 144:160] = jnp.where(sub == 15, halo_f[1, pl.ds(n + 7, 1), :], first).astype(BF16)
+
+    def take_columns(base, copies):
         for c in copies:
             c.wait()
         s2 = base // 8 * 2
         halo_f[0, 8:136, :] = halo_b[s2 + 1].astype(F32) * left_ok
         halo_f[1, 8:136, :] = halo_b[s2 + 0].astype(F32) * right_ok
 
-        def step(n, c):
-            edge(x, n)
-            return c
-
-        lax.fori_loop(1, 129, step, 0, unroll=8)
-
-    def finish_rows(x, base, copies):
-        for c in copies:
-            c.wait()
+    def take_corners(base):
         s4 = base // 8 * 4
         halo_f[0, 0:8, :] = corner_in[s4 + 3] * (left_ok * up_ok)
         halo_f[1, 0:8, :] = corner_in[s4 + 2] * (right_ok * up_ok)
         halo_f[0, 136:144, :] = corner_in[s4 + 1] * (left_ok * down_ok)
         halo_f[1, 136:144, :] = corner_in[s4 + 0] * (right_ok * down_ok)
 
+    put_corners(0)
+    mid = pl.ds(16, 128)
+    rows1 = row_copies(
+        [(row_out.at[0], rows_halo.at[1, mid]), (row_out.at[1], rows_halo.at[0, mid])], 0
+    ) + corner_copies(0)
+    cols1 = col_copies(0)
+    for c in rows1 + cols1:
+        c.start()
+
+    hi, low, _ = split3(cell)
+    tapped = jnp.dot(jnp.concatenate([hi, low], axis=1), wtap[...], preferred_element_type=F32)
+    for n in range(9):
+        patch[n] = tapped[:, n * 128 : (n + 1) * 128]
+    for b in range(3):
+        rhs = []
+        for col in range(PATCH):
+            parts = [
+                patch[a * 3 + b, pl.ds(col, 16, stride=PATCH), :] for a in range(3)
+            ]
+            hi, low, _ = split3(jnp.concatenate(parts, axis=0))
+            rhs.append(jnp.concatenate([hi, low, hi], axis=0))
+        got = jnp.dot(
+            lhs_tap_row[...], jnp.concatenate(rhs, axis=1), preferred_element_type=F32
+        )
+        for col in range(PATCH):
+            taps[pl.ds(b * 16 + col, 128, stride=48), :] = got[:, col * 128 : (col + 1) * 128]
+
+    def sum_up(carry, v):
+        total, square = carry
+        v3 = v.reshape(v.shape[0] // 8, 8, 128)
+        return total + jnp.sum(v3, axis=0), square + jnp.sum(v3 * v3, axis=0)
+
+    def add_taps(n, carry):
+        rhs = []
+        for q in range(16):
+            h = n * 16 + q
+            hi, low, _ = split3(taps[pl.ds(pl.multiple_of(h * 48, 16), 48), :])
+            rhs.append(jnp.concatenate([hi, low, hi], axis=0))
+        got = jnp.dot(
+            lhs_tap_col[...], jnp.concatenate(rhs, axis=1), preferred_element_type=F32
+        )
+        for q in range(16):
+            h = n * 16 + q
+            v = field[at_row(h), :] + got[:, q * 128 : (q + 1) * 128]
+            field[at_row(h), :] = v
+            carry = sum_up(carry, v)
+        return carry
+
+    zero8 = jnp.zeros((8, 128), F32)
+    sums = lax.fori_loop(0, 8, add_taps, (zero8, zero8))
+
+    def correct(carry, place, delta):
+        old = field[place, :]
+        new = old + delta
+        field[place, :] = new
+        d3 = delta.reshape(16, 8, 128)
+        q3 = (new * new - old * old).reshape(16, 8, 128)
+        return carry[0] + jnp.sum(d3, axis=0), carry[1] + jnp.sum(q3, axis=0)
+
+    def take_rows1():
+        for c in rows1:
+            c.wait()
+        for side, ok in ((0, up_ok), (1, down_ok)):
+            v = rows_halo[side, 16:144].astype(F32) * ok
+            rows_halo[side, 16:144] = v.astype(BF16)
+            last = pltpu.roll(v[112:128], 1, 0)
+            rows_halo[side, 0:16] = jnp.where(sub == 0, 0.0, last).astype(BF16)
+            first = pltpu.roll(v[0:16], 15, 0)
+            rows_halo[side, 144:160] = jnp.where(sub == 15, 0.0, first).astype(BF16)
+
+    take_columns(0, cols1)
+    take_rows1()
+    take_corners(0)
+    for side in range(2):
+        lhs = jnp.concatenate([halo_f[side, 7 + a : 135 + a, :].astype(BF16) for a in range(3)], axis=1)
+        rhs = jnp.concatenate([k1[a, 2 * side] for a in range(3)], axis=0)
+        delta = jnp.dot(lhs, rhs, preferred_element_type=F32)
+        sums = correct(sums, pl.ds(side * 127, 128, stride=128), delta)
+    for side in range(2):
+        lhs = jnp.concatenate([rows_halo[side, b * 16 : b * 16 + 128] for b in range(3)], axis=1)
+        rhs = jnp.concatenate([k1[2 * side, b] for b in range(3)], axis=0)
+        delta = jnp.dot(lhs, rhs, preferred_element_type=F32)
+        sums = correct(sums, pl.ds(side * 127 * 128, 128), delta)
+
+    def convolve(columns, rows):
+        def step(t, carry):
+            for h, v in conv_block(x2, wb2, t):
+                field[at_row(h), :] = v
+                carry = sum_up(carry, v)
+            return carry
+
+        def edges(n, c):
+            edge(x2, n)
+            return c
+
+        blocks = 64 // PAIRS
+        take_columns(8, columns)
+        lax.fori_loop(1, 129, edges, 0, unroll=8)
+        sums = lax.fori_loop(1, blocks - 1, step, (zero8, zero8))
+        for c in rows:
+            c.wait()
+        take_corners(8)
+
         @pl.when(i == 0)
         def _():
-            x[0, 1:9] = jnp.zeros((8, 16, 128), BF16)
+            x2[0, 16:144] = jnp.zeros((128, 128), BF16)
 
         @pl.when(i == 7)
         def _():
-            x[129, 1:9] = jnp.zeros((8, 16, 128), BF16)
-
-        edge(x, 0)
-        edge(x, 129)
-
-    mix_rows(0, 2)
-    mix_rows(126, 2)
-    halo1 = row_copies(x1, 0) + corner_copies(0)
-    put_corners(0)
-    for c in halo1:
-        c.start()
-
-    def mix_loop(n, c):
-        mix_rows(2 + n * 32, 32)
-        return c
-
-    lax.fori_loop(0, 3, mix_loop, 0)
-    mix_rows(98, 28)
-    put_columns(0)
-    cols1 = col_copies(0)
-    for c in cols1:
-        c.start()
-
-    def convolve(x, wb, base, columns, rows):
-        def step(t, carry):
-            total, square = carry
-            y = t * (2 * PAIRS)
-            lhs = []
-            for q in range(PAIRS):
-                parts = [
-                    x[y + 2 * q + a, b : b + 8].reshape(128, 128) for a in range(4) for b in range(3)
-                ]
-                lhs.append(jnp.concatenate(parts, axis=1))
-            got = jnp.dot(jnp.concatenate(lhs, axis=0), wb[...], preferred_element_type=F32)
-            for q in range(PAIRS):
-                for e in range(2):
-                    v = got[q * 128 : (q + 1) * 128, e * 128 : (e + 1) * 128]
-                    field[y + 2 * q + e] = v
-                    v3 = v.reshape(16, 8, 128)
-                    total = total + jnp.sum(v3, axis=0)
-                    square = square + jnp.sum(v3 * v3, axis=0)
-            return total, square
-
-        blocks = 64 // PAIRS
-        zero = jnp.zeros((8, 128), F32)
-        finish_columns(x, base, columns)
-        sums = lax.fori_loop(1, blocks - 1, step, (zero, zero))
-        finish_rows(x, base, rows)
+            x2[129, 16:144] = jnp.zeros((128, 128), BF16)
+
+        edge(x2, 0)
+        edge(x2, 129)
         return lax.fori_loop(0, 2, lambda n, c: step(n * (blocks - 1), c), sums)
 
     group_ones = jnp.where(r_iota // 4 == l_iota // 4, 1.0, 0.0)
     number = float(TILE * TILE * 32 * (C // GROUPS))
 
-    def norm_terms(n, sums, gain, shift):
+    def norm_terms(n, sums, gain, shift, meanwhile=None):
         total, square = (jnp.sum(s, axis=0, keepdims=True) for s in sums)
         sub8 = lax.broadcasted_iota(jnp.int32, (8, 128), 0)
         mine = jnp.where(sub8 == 0, total, jnp.where(sub8 == 1, square, 0.0))
@@ -409,6 +559,8 @@
             return c
 
         lax.fori_loop(96, 127, send, 0)
+        if meanwhile is not None:
+            meanwhile()
         whole(st_in.at[n, pl.ds(1, 31)], st_sem.at[n, 1]).wait()
         both = jnp.sum(st_in[n], axis=0)
         both = jnp.dot(
@@ -420,13 +572,12 @@
         whole(st_in.at[n, pl.ds(1, 31)], st_sem.at[n, 0]).wait()
         return scale, shift - mean * scale
 
-    sums = convolve(x1, wb1, 0, cols1, halo1)
-    scale, offset = norm_terms(0, sums, g1_ref[...], s1_ref[...])
+    scale, offset = norm_terms(0, sums, g1_ref[...], s1_ref[...], form_mixed)
 
     def hide(h, lo, hi):
-        v = field[h, lo * 16 : hi * 16, :]
+        v = field[pl.ds(pl.multiple_of(h * 128 + lo * 16, 16), (hi - lo) * 16), :]
         m = silu(v * scale + offset).astype(BF16)
-        x2[h + 1, 1 + lo : 1 + hi] = m.reshape(hi - lo, 16, 128)
+        x2[h + 1, 16 + lo * 16 : 16 + hi * 16] = m
         return m.astype(F32)
 
     def hide_ends(h, c):
@@ -447,20 +598,22 @@
         c.start()
     hide_rest(0, 0)
     hide_rest(127, 0)
-    halo2 = row_copies(x2, 8) + corner_copies(8)
+    halo2 = row_copies(
+        [(x2.at[1, mid], x2.at[129, mid]), (x2.at[128, mid], x2.at[0, mid])], 8
+    ) + corner_copies(8)
     put_corners(8)
     for c in halo2:
         c.start()
     lax.fori_loop(1, 127, hide_rest, 0, unroll=7)
 
-    sums = convolve(x2, wb2, 8, cols2, halo2)
+    sums = convolve(cols2, halo2)
     scale2, offset2 = norm_terms(1, sums, g2_ref[...], s2_ref[...])
 
     def finish(n, c):
         for q in range(8):
             h = n * 8 + q
-            v = silu(field[h] * scale2 + offset2)
-            v = x1[h + 1, 1:9].reshape(128, 128).astype(F32) + v
+            v = silu(field[at_row(h), :] * scale2 + offset2)
+            v = mixed[h].astype(F32) + v
             for s in range(8):
                 swap[q, pl.ds(s, 16, stride=8), :] = v[s * 16 : (s + 1) * 16]
         for q in range(8):
@@ -510,12 +663,20 @@
             pltpu.VMEM((128, MOST, C), F32),
             pltpu.VMEM((8, 256), jnp.int32),
             pltpu.VMEM((256, MOST * 128), BF16),
-            pltpu.VMEM((256, C), F32),
+            pltpu.VMEM((10, 256, C), F32),
             pltpu.VMEM((TILE * 16, C), F32),
+            pltpu.VMEM((2, 128, C), BF16),
+            pltpu.VMEM((TILE * 48, C), F32),
             pltpu.VMEM((128, 256), BF16),
-            pltpu.VMEM((TILE + 2, 10, 16, C), BF16),
-            pltpu.VMEM((TILE + 2, 10, 16, C), BF16),
-            pltpu.VMEM((TILE, TILE, C), F32),
+            pltpu.VMEM((128, 144), BF16),
+            pltpu.VMEM((128, 144), BF16),
+            pltpu.VMEM((64, 256), F32),
+            pltpu.VMEM((2, 128, C), F32),
+            pltpu.VMEM((256, 9 * C), BF16),
+            pltpu.VMEM((2, 160, C), BF16),
+            pltpu.VMEM((TILE, TILE, C), BF16),
+            pltpu.VMEM((TILE + 2, 160, C), BF16),
+            pltpu.VMEM((TILE * TILE, C), F32),
             pltpu.VMEM((8, TILE, C), F32),
             pltpu.VMEM((2, TILE, C), F32),
             pltpu.VMEM((4, TILE, C), BF16),
@@ -546,7 +707,7 @@
         row(shift_first),
         row(gain_second),
         row(shift_second),
-        request_ids.reshape(128, MOST).T,
+        request_ids.transpose(0, 1, 4, 2, 3).reshape(MOST, 1, 128),
         patch_slots.reshape(1, PATCH * PATCH),
         tile_offsets.reshape(1, 2),
     )

time: 68.4 us -> 61.5 us (0.90)
  Pallas kernels: 64.9 us -> 59.4 us
  local copies, waits for them, and re-layouts: 3.29 us -> 2.02 us
    pallas_call x1, Pallas kernels: 64.9 us -> 59.4 us  [body(): pl.pallas_call(kernel, out_shape=pltpu.VMEM((TILE, TILE, C), BF16), in_sp...]
    unnamed x2 -> x1, local copies, waits for them, and re-layouts: 3.29 us -> 2.02 us
where the time goes in v2:
time: 61.5 us; the launch traced here: 61.4 us
  Pallas kernels  59.4 us (97%)
  local copies, waits for them, and re-layouts  2.02 us (3%)
    pallas_call x1, Pallas kernels, body(): pl.pallas_call(kernel, out_shape=pltpu.VMEM((TILE, TILE, C), BF16), in_sp...  59.4 us
    unnamed x1, local copies, waits for them, and re-layouts  2.02 us

profile of v2, /device:TPU:1, one launch (start us, length us, event | category | flops | bytes accessed | tf_op | source)
XLA Modules:
  0.0 61.4 jit_solution(6106708127935502193)
XLA Ops:
  0.0 59.4 %block.1 = bf16[128,128,128]{2,1,0:T(8,128)(2,1)S(1)} custom-call(bf16[128,128,128]{2,1,0:T(8,128)(2,1)} %bitcast.12, f32[256,640]{1,0:T(8,128)} %cells_hbm.1, f32[640,128]{1,0:T(8,128)} %proj_hbm.1, bf16[3,3,128,128]{3,2,1,0:T(8,128)(2,1)} %k1_hbm.1, bf16[3,3,128,128]{3,2,1,0:T(8,128)(2,1)} %k2_hbm.1, f32[1,128]{1,0:T(1,128)} %bitcast.15, ...), custom_call_target="tpu_custom_call" | custom-call | tf_op jit(solution)/shard_map/block/pallas_call | solution.py:645
  59.4 2.0 %copy.14 = bf16[1,128,128,128]{3,2,1,0:T(8,128)(2,1)} copy(bf16[1,128,128,128]{3,2,1,0:T(8,128)(2,1)S(1)} %bitcast.11) | data formatting | bytes 8388608

commit v3 on v2

--- a/solution.py
+++ b/solution.py
@@ -29,6 +29,11 @@
     mid = rest.astype(BF16)
     lo = (rest - mid.astype(F32)).astype(BF16)
     return hi, mid, lo
+
+
+def split2(x):
+    hi = x.astype(BF16)
+    return hi, (x - hi.astype(F32)).astype(BF16)
 
 
 def cubic(distance):
@@ -103,7 +108,7 @@
     lhs_col,
     lhs_tap_row,
     lhs_tap_col,
-    edge_sel,
+    edge_rows,
     noisy_col,
     wtap,
     rows_halo,
@@ -165,7 +170,7 @@
     projected = jnp.dot(
         cells[...], proj[...], precision=lax.Precision.HIGHEST, preferred_element_type=F32
     )
-    for n, term in enumerate(split3(projected)):
+    for n, term in enumerate(split2(projected)):
         pcat[:, n * 128 : (n + 1) * 128] = term
     partial[...] = jnp.zeros_like(partial)
     taps[...] = jnp.zeros_like(taps)
@@ -202,7 +207,8 @@
     position = (start.astype(F32) + point.astype(F32) * STEP) / 128.0 + 1.0
     weight = cubic(jnp.abs(position - jnp.where(on_rows, p_row, p_col).astype(F32)))
     keep = (jnp.where(on_rows, p_col, p_row) == (e_row & 15)) & (p_cell < PATCH * PATCH)
-    edge_sel[...] = jnp.where(keep, weight, 0.0)
+    edge_terms = jnp.concatenate(split2(jnp.where(keep, weight, 0.0)), axis=0)
+    edge_rows[...] = jnp.dot(edge_terms, sel[...], preferred_element_type=F32).astype(BF16)
 
     loads[2].wait()
     loads[3].wait()
@@ -271,11 +277,13 @@
     whole(id_recv.at[pl.ds(1, 127)], id_sem.at[1]).wait()
     asked = id_recv[:, 0, :] - (me * HELD).astype(F32)
     row_iota = lax.broadcasted_iota(jnp.int32, (128, HELD), 1).astype(F32)
+    hot = [
+        jnp.where(asked[:, m : m + 1] == row_iota, 1.0, 0.0).astype(BF16) for m in range(MOST)
+    ]
+    found = jnp.dot(jnp.concatenate(hot, axis=0), pcat[...], preferred_element_type=F32)
+    found = found[:, 0:128] + found[:, 128:256]
     for m in range(MOST):
-        hot = jnp.where(asked[:, m : m + 1] == row_iota, 1.0, 0.0).astype(BF16)
-        found = jnp.dot(hot, pcat[...], preferred_element_type=F32)
-        found = found[:, 0:128] + found[:, 128:256] + found[:, 256:384]
-        rows_out[:, m, :] = found
+        rows_out[:, m, :] = found[m * 128 : (m + 1) * 128]
     rows_in[0] = rows_out[0]
 
     def send_rows(n, c):
@@ -295,19 +303,17 @@
     whole(id_buf.at[pl.ds(1, 127)], id_sem.at[0]).wait()
     whole(rows_in.at[pl.ds(1, 127)], row_sem.at[1]).wait()
 
-    terms = [jnp.concatenate(split3(rows_in[:, m, :]), axis=1) for m in range(MOST)]
-    cell = jnp.dot(sel[...], jnp.concatenate(terms, axis=0), preferred_element_type=F32)
-    cell = cell[:, 0:128] + cell[:, 128:256] + cell[:, 256:384]
-    patch[9] = cell
+    terms = [jnp.concatenate(split2(rows_in[:, m, :]), axis=1) for m in range(MOST)]
+    terms = jnp.concatenate(terms, axis=0)
     zero_tile = jnp.zeros((32, 128), BF16)
 
     def stack_terms(x):
         hi, mid, lo = split3(x)
         return jnp.concatenate([hi, mid, lo, hi, mid, hi, zero_tile], axis=0)
 
-    ends = jnp.dot(
-        edge_sel[...], cell, precision=lax.Precision.HIGHEST, preferred_element_type=F32
-    )
+    got = jnp.dot(edge_rows[...], terms, preferred_element_type=F32)
+    got = got[:, 0:128] + got[:, 128:256]
+    ends = got[0:64] + got[64:128]
     for side in range(2):
         h = side * (TILE - 1)
         rhs = jnp.concatenate([stack_terms(ends[side * 16 : side * 16 + 16]), noisy[h]], axis=0)
@@ -402,12 +408,6 @@
     up_ok = jnp.where(i > 0, 1.0, 0.0)
     down_ok = jnp.where(i < 7, 1.0, 0.0)
 
-    def edge(x, n):
-        last = pltpu.roll(x[n, 128:144].astype(F32), 1, 0)
-        x[n, 0:16] = jnp.where(sub == 0, halo_f[0, pl.ds(n + 7, 1), :], last).astype(BF16)
-        first = pltpu.roll(x[n, 16:32].astype(F32), 15, 0)
-        x[n, 144:160] = jnp.where(sub == 15, halo_f[1, pl.ds(n + 7, 1), :], first).astype(BF16)
-
     def take_columns(base, copies):
         for c in copies:
             c.wait()
@@ -428,10 +428,13 @@
         [(row_out.at[0], rows_halo.at[1, mid]), (row_out.at[1], rows_halo.at[0, mid])], 0
     ) + corner_copies(0)
     cols1 = col_copies(0)
-    for c in rows1 + cols1:
+    for c in rows1[2:] + rows1[:2] + cols1:
         c.start()
 
-    hi, low, _ = split3(cell)
+    cell = jnp.dot(sel[...], terms, preferred_element_type=F32)
+    cell = cell[:, 0:128] + cell[:, 128:256]
+    patch[9] = cell
+    hi, low = split2(cell)
     tapped = jnp.dot(jnp.concatenate([hi, low], axis=1), wtap[...], preferred_element_type=F32)
     for n in range(9):
         patch[n] = tapped[:, n * 128 : (n + 1) * 128]
@@ -441,7 +444,7 @@
             parts = [
                 patch[a * 3 + b, pl.ds(col, 16, stride=PATCH), :] for a in range(3)
             ]
-            hi, low, _ = split3(jnp.concatenate(parts, axis=0))
+            hi, low = split2(jnp.concatenate(parts, axis=0))
             rhs.append(jnp.concatenate([hi, low, hi], axis=0))
         got = jnp.dot(
             lhs_tap_row[...], jnp.concatenate(rhs, axis=1), preferred_element_type=F32
@@ -458,7 +461,7 @@
         rhs = []
         for q in range(16):
             h = n * 16 + q
-            hi, low, _ = split3(taps[pl.ds(pl.multiple_of(h * 48, 16), 48), :])
+            hi, low = split2(taps[pl.ds(pl.multiple_of(h * 48, 16), 48), :])
             rhs.append(jnp.concatenate([hi, low, hi], axis=0))
         got = jnp.dot(
             lhs_tap_col[...], jnp.concatenate(rhs, axis=1), preferred_element_type=F32
@@ -481,61 +484,32 @@
         q3 = (new * new - old * old).reshape(16, 8, 128)
         return carry[0] + jnp.sum(d3, axis=0), carry[1] + jnp.sum(q3, axis=0)
 
-    def take_rows1():
-        for c in rows1:
-            c.wait()
-        for side, ok in ((0, up_ok), (1, down_ok)):
-            v = rows_halo[side, 16:144].astype(F32) * ok
-            rows_halo[side, 16:144] = v.astype(BF16)
-            last = pltpu.roll(v[112:128], 1, 0)
-            rows_halo[side, 0:16] = jnp.where(sub == 0, 0.0, last).astype(BF16)
-            first = pltpu.roll(v[0:16], 15, 0)
-            rows_halo[side, 144:160] = jnp.where(sub == 15, 0.0, first).astype(BF16)
-
-    take_columns(0, cols1)
-    take_rows1()
-    take_corners(0)
-    for side in range(2):
-        lhs = jnp.concatenate([halo_f[side, 7 + a : 135 + a, :].astype(BF16) for a in range(3)], axis=1)
-        rhs = jnp.concatenate([k1[a, 2 * side] for a in range(3)], axis=0)
-        delta = jnp.dot(lhs, rhs, preferred_element_type=F32)
-        sums = correct(sums, pl.ds(side * 127, 128, stride=128), delta)
-    for side in range(2):
-        lhs = jnp.concatenate([rows_halo[side, b * 16 : b * 16 + 128] for b in range(3)], axis=1)
-        rhs = jnp.concatenate([k1[2 * side, b] for b in range(3)], axis=0)
-        delta = jnp.dot(lhs, rhs, preferred_element_type=F32)
-        sums = correct(sums, pl.ds(side * 127 * 128, 128), delta)
-
-    def convolve(columns, rows):
-        def step(t, carry):
-            for h, v in conv_block(x2, wb2, t):
-                field[at_row(h), :] = v
-                carry = sum_up(carry, v)
-            return carry
-
-        def edges(n, c):
-            edge(x2, n)
-            return c
-
-        blocks = 64 // PAIRS
-        take_columns(8, columns)
-        lax.fori_loop(1, 129, edges, 0, unroll=8)
-        sums = lax.fori_loop(1, blocks - 1, step, (zero8, zero8))
+    def add_borders(base, rows, columns, k, carry):
+        n = base // 8 * 2
+        take_columns(base, columns)
         for c in rows:
             c.wait()
-        take_corners(8)
-
-        @pl.when(i == 0)
-        def _():
-            x2[0, 16:144] = jnp.zeros((128, 128), BF16)
-
-        @pl.when(i == 7)
-        def _():
-            x2[129, 16:144] = jnp.zeros((128, 128), BF16)
-
-        edge(x2, 0)
-        edge(x2, 129)
-        return lax.fori_loop(0, 2, lambda n, c: step(n * (blocks - 1), c), sums)
+        take_corners(base)
+        for side, ok in ((0, up_ok), (1, down_ok)):
+            v = rows_halo[n + side, 16:144].astype(F32) * ok
+            rows_halo[n + side, 16:144] = v.astype(BF16)
+            last = pltpu.roll(v[112:128], 1, 0)
+            rows_halo[n + side, 0:16] = jnp.where(sub == 0, 0.0, last).astype(BF16)
+            first = pltpu.roll(v[0:16], 15, 0)
+            rows_halo[n + side, 144:160] = jnp.where(sub == 15, 0.0, first).astype(BF16)
+        for side in range(2):
+            lhs = [halo_f[side, 7 + a : 135 + a, :].astype(BF16) for a in range(3)]
+            rhs = jnp.concatenate([k[a, 2 * side] for a in range(3)], axis=0)
+            delta = jnp.dot(jnp.concatenate(lhs, axis=1), rhs, preferred_element_type=F32)
+            carry = correct(carry, pl.ds(side * 127, 128, stride=128), delta)
+        for side in range(2):
+            lhs = [rows_halo[n + side, b * 16 : b * 16 + 128] for b in range(3)]
+            rhs = jnp.concatenate([k[2 * side, b] for b in range(3)], axis=0)
+            delta = jnp.dot(jnp.concatenate(lhs, axis=1), rhs, preferred_element_type=F32)
+            carry = correct(carry, pl.ds(side * 127 * 128, 128), delta)
+        return carry
+
+    sums = add_borders(0, rows1, cols1, k1, sums)
 
     group_ones = jnp.where(r_iota // 4 == l_iota // 4, 1.0, 0.0)
     number = float(TILE * TILE * 32 * (C // GROUPS))
@@ -574,39 +548,38 @@
 
     scale, offset = norm_terms(0, sums, g1_ref[...], s1_ref[...], form_mixed)
 
-    def hide(h, lo, hi):
-        v = field[pl.ds(pl.multiple_of(h * 128 + lo * 16, 16), (hi - lo) * 16), :]
-        m = silu(v * scale + offset).astype(BF16)
-        x2[h + 1, 16 + lo * 16 : 16 + hi * 16] = m
-        return m.astype(F32)
-
-    def hide_ends(h, c):
-        a = hide(h, 0, 1)
-        b = hide(h, 7, 8)
-        col_f[0, pl.ds(h, 1), :] = a[0:1]
-        col_f[1, pl.ds(h, 1), :] = b[15:16]
-        return c
-
-    def hide_rest(h, c):
-        hide(h, 1, 7)
-        return c
-
-    lax.fori_loop(0, 128, hide_ends, 0, unroll=8)
-    put_columns(8)
+    def hide(place):
+        return silu(field[place, :] * scale + offset)
+
+    for side in range(2):
+        col_b[2 + side] = hide(pl.ds(side * 127, 128, stride=128)).astype(BF16)
+        col_f[side] = col_b[2 + side].astype(F32)
+        row_out[2 + side] = hide(pl.ds(side * 127 * 128, 128)).astype(BF16)
+    put_corners(8)
+    rows2 = row_copies(
+        [(row_out.at[2], rows_halo.at[3, mid]), (row_out.at[3], rows_halo.at[2, mid])], 8
+    ) + corner_copies(8)
     cols2 = col_copies(8)
-    for c in cols2:
+    for c in rows2[2:] + rows2[:2] + cols2:
         c.start()
-    hide_rest(0, 0)
-    hide_rest(127, 0)
-    halo2 = row_copies(
-        [(x2.at[1, mid], x2.at[129, mid]), (x2.at[128, mid], x2.at[0, mid])], 8
-    ) + corner_copies(8)
-    put_corners(8)
-    for c in halo2:
-        c.start()
-    lax.fori_loop(1, 127, hide_rest, 0, unroll=7)
-
-    sums = convolve(cols2, halo2)
+
+    def hide_row(h):
+        v = hide(pl.ds(h * 128, 128))
+        x2[h + 1, 16:144] = v.astype(BF16)
+        x2[h + 1, 0:16] = jnp.where(sub == 0, 0.0, pltpu.roll(v[112:128], 1, 0)).astype(BF16)
+        x2[h + 1, 144:160] = jnp.where(sub == 15, 0.0, pltpu.roll(v[0:16], 15, 0)).astype(BF16)
+
+    many = 2 * PAIRS
+    for h in range(many + 1):
+        hide_row(h)
+    sums = (zero8, zero8)
+    for t in range(TILE // many):
+        for h in range((t + 1) * many + 1, min((t + 2) * many + 1, TILE)):
+            hide_row(h)
+        for h, v in conv_block(x2, wb2, t):
+            field[pl.ds(h * 128, 128), :] = v
+            sums = sum_up(sums, v)
+    sums = add_borders(8, rows2, cols2, k2, sums)
     scale2, offset2 = norm_terms(1, sums, g2_ref[...], s2_ref[...])
 
     def finish(n, c):
@@ -658,22 +631,22 @@
             pltpu.VMEM((128, 128), F32),
             pltpu.VMEM((128, 1, 128), F32),
             pltpu.VMEM((128, 1, 128), F32),
-            pltpu.VMEM((HELD, 3 * C), BF16),
+            pltpu.VMEM((HELD, 2 * C), BF16),
             pltpu.VMEM((128, MOST, C), F32),
             pltpu.VMEM((128, MOST, C), F32),
             pltpu.VMEM((8, 256), jnp.int32),
             pltpu.VMEM((256, MOST * 128), BF16),
             pltpu.VMEM((10, 256, C), F32),
             pltpu.VMEM((TILE * 16, C), F32),
-            pltpu.VMEM((2, 128, C), BF16),
+            pltpu.VMEM((4, 128, C), BF16),
             pltpu.VMEM((TILE * 48, C), F32),
             pltpu.VMEM((128, 256), BF16),
             pltpu.VMEM((128, 144), BF16),
             pltpu.VMEM((128, 144), BF16),
-            pltpu.VMEM((64, 256), F32),
+            pltpu.VMEM((128, MOST * 128), BF16),
             pltpu.VMEM((2, 128, C), F32),
             pltpu.VMEM((256, 9 * C), BF16),
-            pltpu.VMEM((2, 160, C), BF16),
+            pltpu.VMEM((4, 160, C), BF16),
             pltpu.VMEM((TILE, TILE, C), BF16),
             pltpu.VMEM((TILE + 2, 160, C), BF16),
             pltpu.VMEM((TILE * TILE, C), F32),

time: 61.5 us -> 57.1 us (0.928)
  Pallas kernels: 59.4 us -> 54.9 us
    pallas_call x1, Pallas kernels: 59.4 us -> 54.9 us  [body(): pl.pallas_call(kernel, out_shape=pltpu.VMEM((TILE, TILE, C), BF16), in_sp...]
where the time goes in v3:
time: 57.1 us; the launch traced here: 57 us
  Pallas kernels  54.9 us (96%)
  local copies, waits for them, and re-layouts  2.02 us (4%)
    pallas_call x1, Pallas kernels, body(): pl.pallas_call(kernel, out_shape=pltpu.VMEM((TILE, TILE, C), BF16), in_sp...  54.9 us
    unnamed x1, local copies, waits for them, and re-layouts  2.02 us

profile of v3, /device:TPU:1, one launch (start us, length us, event | category | flops | bytes accessed | tf_op | source)
XLA Modules:
  0.0 57.0 jit_solution(6807513983907215156)
XLA Ops:
  0.0 54.9 %block.1 = bf16[128,128,128]{2,1,0:T(8,128)(2,1)S(1)} custom-call(bf16[128,128,128]{2,1,0:T(8,128)(2,1)} %bitcast.12, f32[256,640]{1,0:T(8,128)} %cells_hbm.1, f32[640,128]{1,0:T(8,128)} %proj_hbm.1, bf16[3,3,128,128]{3,2,1,0:T(8,128)(2,1)} %k1_hbm.1, bf16[3,3,128,128]{3,2,1,0:T(8,128)(2,1)} %k2_hbm.1, f32[1,128]{1,0:T(1,128)} %bitcast.15, ...), custom_call_target="tpu_custom_call" | custom-call | tf_op jit(solution)/shard_map/block/pallas_call | solution.py:618
  55.0 2.0 %copy.14 = bf16[1,128,128,128]{3,2,1,0:T(8,128)(2,1)} copy(bf16[1,128,128,128]{3,2,1,0:T(8,128)(2,1)S(1)} %bitcast.11) | data formatting | bytes 8388608

commit v4 on v3

--- a/solution.py
+++ b/solution.py
@@ -85,7 +85,9 @@
     ids_ref,
     slots_ref,
     off_ref,
-    out,
+    field,
+    mixed,
+    terms_out,
     noisy,
     cells,
     proj,
@@ -112,10 +114,7 @@
     noisy_col,
     wtap,
     rows_halo,
-    mixed,
     x2,
-    field,
-    swap,
     col_f,
     col_b,
     halo_b,
@@ -582,19 +581,30 @@
     sums = add_borders(8, rows2, cols2, k2, sums)
     scale2, offset2 = norm_terms(1, sums, g2_ref[...], s2_ref[...])
 
+    terms_out[0:1, :] = scale2
+    terms_out[1:2, :] = offset2
+    whole(rows_in.at[pl.ds(1, 127)], row_sem.at[0]).wait()
+
+
+def result_kernel(field, mixed, terms, out_hbm, stage, swap, sem):
+    scale = terms[0:1, :]
+    offset = terms[1:2, :]
+
     def finish(n, c):
         for q in range(8):
             h = n * 8 + q
-            v = silu(field[at_row(h), :] * scale2 + offset2)
+            v = silu(field[pl.ds(pl.multiple_of(h * 128, 128), 128), :] * scale + offset)
             v = mixed[h].astype(F32) + v
             for s in range(8):
                 swap[q, pl.ds(s, 16, stride=8), :] = v[s * 16 : (s + 1) * 16]
         for q in range(8):
-            out[n * 8 + q] = swap[q].astype(BF16)
+            stage[n * 8 + q] = swap[q].astype(BF16)
+        rows = pl.ds(n * 8, 8)
+        pltpu.make_async_copy(stage.at[rows], out_hbm.at[rows], sem).start()
         return c
 
     lax.fori_loop(0, 16, finish, 0)
-    whole(rows_in.at[pl.ds(1, 127)], row_sem.at[0]).wait()
+    pltpu.make_async_copy(stage, out_hbm, sem).wait()
 
 
 def body(
@@ -615,11 +625,15 @@
     vmem = pl.BlockSpec(memory_space=pltpu.VMEM)
     smem = pl.BlockSpec(memory_space=pltpu.SMEM)
     row = lambda v: v.reshape(1, C)
-    got = pl.pallas_call(
+    second, mixed, terms = pl.pallas_call(
         kernel,
-        out_shape=pltpu.VMEM((TILE, TILE, C), BF16),
+        out_shape=[
+            pltpu.VMEM((TILE * TILE, C), F32),
+            pltpu.VMEM((TILE, TILE, C), BF16),
+            pltpu.VMEM((8, C), F32),
+        ],
         in_specs=[hbm] * 5 + [vmem] * 6 + [smem],
-        out_specs=vmem,
+        out_specs=[vmem] * 3,
         scratch_shapes=[
             pltpu.VMEM((TILE, TILE, C), BF16),
             pltpu.VMEM((HELD, CC), F32),
@@ -647,10 +661,7 @@
             pltpu.VMEM((2, 128, C), F32),
             pltpu.VMEM((256, 9 * C), BF16),
             pltpu.VMEM((4, 160, C), BF16),
-            pltpu.VMEM((TILE, TILE, C), BF16),
             pltpu.VMEM((TILE + 2, 160, C), BF16),
-            pltpu.VMEM((TILE * TILE, C), F32),
-            pltpu.VMEM((8, TILE, C), F32),
             pltpu.VMEM((2, TILE, C), F32),
             pltpu.VMEM((4, TILE, C), BF16),
             pltpu.VMEM((4, TILE, C), BF16),
@@ -667,7 +678,7 @@
             pltpu.SemaphoreType.DMA((16,)),
         ],
         compiler_params=pltpu.CompilerParams(
-            collective_id=0, has_side_effects=True, vmem_limit_bytes=59 << 20
+            collective_id=0, has_side_effects=True, vmem_limit_bytes=50 << 20
         ),
         name="block",
     )(
@@ -684,6 +695,19 @@
         patch_slots.reshape(1, PATCH * PATCH),
         tile_offsets.reshape(1, 2),
     )
+    got = pl.pallas_call(
+        result_kernel,
+        out_shape=jax.ShapeDtypeStruct((TILE, TILE, C), BF16),
+        in_specs=[vmem] * 3,
+        out_specs=hbm,
+        scratch_shapes=[
+            pltpu.VMEM((TILE, TILE, C), BF16),
+            pltpu.VMEM((8, TILE, C), F32),
+            pltpu.SemaphoreType.DMA,
+        ],
+        compiler_params=pltpu.CompilerParams(vmem_limit_bytes=10 << 20),
+        name="result",
+    )(second, mixed, terms)
     return got[None]
 
 

time: 57.1 us -> 55.8 us (0.977)
  local copies, waits for them, and re-layouts: 2.02 us -> 0 us
  Pallas kernels: 54.9 us -> 55.5 us
    unnamed x1 -> x0, local copies, waits for them, and re-layouts: 2.02 us -> none
    pallas_call x1 -> x2, Pallas kernels: 54.9 us -> 55.5 us  [the longest x1 52.3 us: body(): pl.pallas_call(kernel, out_shape=[pltpu.VMEM((TILE * TILE, C), F32), pltp...]
where the time goes in v4:
time: 55.8 us; the launch traced here: 55.6 us
  Pallas kernels  55.5 us (99%)
    pallas_call x1, Pallas kernels, body(): pl.pallas_call(kernel, out_shape=[pltpu.VMEM((TILE * TILE, C), F32), pltp...  52.3 us
    pallas_call x1, Pallas kernels, body(): pl.pallas_call(result_kernel, out_shape=jax.ShapeDtypeStruct((TILE, TILE,...  3.17 us

profile of v4, /device:TPU:1, one launch (start us, length us, event | category | flops | bytes accessed | tf_op | source)
XLA Modules:
  0.0 55.6 jit_solution(11444915593702024343)
XLA Ops:
  0.0 52.3 %block.1 = (f32[16384,128]{1,0:T(8,128)S(1)}, bf16[128,128,128]{2,1,0:T(8,128)(2,1)S(1)}, f32[8,128]{1,0:T(8,128)S(1)}) custom-call(bf16[128,128,128]{2,1,0:T(8,128)(2,1)} %bitcast.11, f32[256,640]{1,0:T(8,128)} %cells_hbm.1, f32[640,128]{1,0:T(8,128)} %proj_hbm.1, bf16[3,3,128,128]{3,2,1,0:T(8,128)(2,1)} %k1_hbm.1, bf16[3,3,128,128]{3,2,1,0:T(8,128)(2,1)} %k2_hbm.1, ...), custom_call_target="tpu_custom_call" | custom-call | tf_op jit(solution)/shard_map/block/pallas_call | solution.py:628
  52.3 3.2 %result.1 = bf16[128,128,128]{2,1,0:T(8,128)(2,1)} custom-call(f32[16384,128]{1,0:T(8,128)S(1)} %get-tuple-element.8.field, bf16[128,128,128]{2,1,0:T(8,128)(2,1)S(1)} %get-tuple-element.9.mixed, f32[8,128]{1,0:T(8,128)S(1)} %get-tuple-element.10.terms), custom_call_target="tpu_custom_call" | custom-call | tf_op jit(solution)/shard_map/result/pallas_call | solution.py:698

commit v5 on v4

--- a/solution.py
+++ b/solution.py
@@ -78,16 +78,20 @@
     proj_hbm,
     k1_hbm,
     k2_hbm,
-    g1_ref,
-    s1_ref,
-    g2_ref,
-    s2_ref,
+    g1_hbm,
+    s1_hbm,
+    g2_hbm,
+    s2_hbm,
+    ids_hbm,
+    slots_hbm,
+    off_hbm,
+    field,
+    mixed,
+    terms_out,
+    vectors,
     ids_ref,
     slots_ref,
     off_ref,
-    field,
-    mixed,
-    terms_out,
     noisy,
     cells,
     proj,
@@ -136,11 +140,23 @@
     loads = [
         pltpu.make_async_copy(a, b, ld_sem.at[n])
         for n, (a, b) in enumerate(
-            [(cells_hbm, cells), (proj_hbm, proj), (k1_hbm, k1), (k2_hbm, k2), (noisy_hbm, noisy)]
+            [
+                (cells_hbm, cells),
+                (proj_hbm, proj),
+                (k1_hbm, k1),
+                (k2_hbm, k2),
+                (noisy_hbm, noisy),
+                (ids_hbm, ids_ref),
+                (slots_hbm, slots_ref),
+                (off_hbm, off_ref),
+                (g1_hbm, vectors.at[0]),
+                (s1_hbm, vectors.at[1]),
+                (g2_hbm, vectors.at[2]),
+                (s2_hbm, vectors.at[3]),
+            ]
         )
     ]
-    for c in loads:
-        c.start()
+    loads[5].start()
     barrier = pltpu.get_barrier_semaphore()
 
     def greet(n, c):
@@ -148,6 +164,9 @@
         return c
 
     lax.fori_loop(0, 127, greet, 0)
+    for c in loads[:5] + loads[6:]:
+        c.start()
+    loads[5].wait()
 
     id_rows[...] = jnp.zeros_like(id_rows)
     id_rows[0:MOST, :] = ids_ref[:, 0, :].astype(F32)
@@ -164,15 +183,16 @@
 
     lax.fori_loop(0, 127, send_ids, 0)
 
-    loads[0].wait()
-    loads[1].wait()
+    for n in (0, 1, 6, 7, 8, 9, 10, 11):
+        loads[n].wait()
     projected = jnp.dot(
         cells[...], proj[...], precision=lax.Precision.HIGHEST, preferred_element_type=F32
     )
     for n, term in enumerate(split2(projected)):
         pcat[:, n * 128 : (n + 1) * 128] = term
-    partial[...] = jnp.zeros_like(partial)
-    taps[...] = jnp.zeros_like(taps)
+    for b in range(PATCH, 16):
+        for n in range(3):
+            taps[pl.ds(n * 16 + b, 128, stride=48), :] = jnp.zeros((128, 128), F32)
 
     slot_row[...] = jnp.full_like(slot_row, -1)
     slot_row[0:1, 0 : PATCH * PATCH] = slots_ref[...]
@@ -210,15 +230,16 @@
     edge_rows[...] = jnp.dot(edge_terms, sel[...], preferred_element_type=F32).astype(BF16)
 
     loads[2].wait()
-    loads[3].wait()
     zero_block = jnp.zeros((128, 128), BF16)
-    for w, wb in ((k1, wb1), (k2, wb2)):
+
+    def two_rows(w, wb):
         for a in range(4):
             for b in range(3):
                 for e in range(2):
                     block = w[a - e, b] if 0 <= a - e <= 2 else zero_block
                     wb[(a * 3 + b) * 128 : (a * 3 + b + 1) * 128, e * 128 : (e + 1) * 128] = block
 
+    two_rows(k1, wb1)
     for a in range(3):
         for b in range(3):
             n = a * 3 + b
@@ -508,9 +529,15 @@
             carry = correct(carry, pl.ds(side * 127 * 128, 128), delta)
         return carry
 
+    loads[3].wait()
+    two_rows(k2, wb2)
+    for b in range(PATCH, 16):
+        partial[pl.ds(b, 128, stride=16), :] = jnp.zeros((128, 128), F32)
     sums = add_borders(0, rows1, cols1, k1, sums)
 
-    group_ones = jnp.where(r_iota // 4 == l_iota // 4, 1.0, 0.0)
+    lane8 = lax.broadcasted_iota(jnp.int32, (8, 128), 1)
+    odd = (lane8 & 1) == 1
+    high = (lane8 & 2) == 2
     number = float(TILE * TILE * 32 * (C // GROUPS))
 
     def norm_terms(n, sums, gain, shift, meanwhile=None):
@@ -536,16 +563,15 @@
             meanwhile()
         whole(st_in.at[n, pl.ds(1, 31)], st_sem.at[n, 1]).wait()
         both = jnp.sum(st_in[n], axis=0)
-        both = jnp.dot(
-            both, group_ones, precision=lax.Precision.HIGHEST, preferred_element_type=F32
-        )
+        both = both + jnp.where(odd, pltpu.roll(both, 1, 1), pltpu.roll(both, 127, 1))
+        both = both + jnp.where(high, pltpu.roll(both, 2, 1), pltpu.roll(both, 126, 1))
         mean = both[0:1] / number
         spread = both[1:2] / number - mean * mean
         scale = lax.rsqrt(spread + 1e-05) * gain
         whole(st_in.at[n, pl.ds(1, 31)], st_sem.at[n, 0]).wait()
         return scale, shift - mean * scale
 
-    scale, offset = norm_terms(0, sums, g1_ref[...], s1_ref[...], form_mixed)
+    scale, offset = norm_terms(0, sums, vectors[0], vectors[1], form_mixed)
 
     def hide(place):
         return silu(field[place, :] * scale + offset)
@@ -579,7 +605,7 @@
             field[pl.ds(h * 128, 128), :] = v
             sums = sum_up(sums, v)
     sums = add_borders(8, rows2, cols2, k2, sums)
-    scale2, offset2 = norm_terms(1, sums, g2_ref[...], s2_ref[...])
+    scale2, offset2 = norm_terms(1, sums, vectors[2], vectors[3])
 
     terms_out[0:1, :] = scale2
     terms_out[1:2, :] = offset2
@@ -623,7 +649,6 @@
 ):
     hbm = pl.BlockSpec(memory_space=pl.ANY)
     vmem = pl.BlockSpec(memory_space=pltpu.VMEM)
-    smem = pl.BlockSpec(memory_space=pltpu.SMEM)
     row = lambda v: v.reshape(1, C)
     second, mixed, terms = pl.pallas_call(
         kernel,
@@ -632,9 +657,13 @@
             pltpu.VMEM((TILE, TILE, C), BF16),
             pltpu.VMEM((8, C), F32),
         ],
-        in_specs=[hbm] * 5 + [vmem] * 6 + [smem],
+        in_specs=[hbm] * 12,
         out_specs=[vmem] * 3,
         scratch_shapes=[
+            pltpu.VMEM((4, 1, C), F32),
+            pltpu.VMEM((MOST, 1, 128), jnp.int32),
+            pltpu.VMEM((1, PATCH * PATCH), jnp.int32),
+            pltpu.SMEM((1, 2), jnp.int32),
             pltpu.VMEM((TILE, TILE, C), BF16),
             pltpu.VMEM((HELD, CC), F32),
             pltpu.VMEM((CC, C), F32),
@@ -670,7 +699,7 @@
             pltpu.VMEM((8, 8, C), F32),
             pltpu.VMEM((2, 8, C), F32),
             pltpu.VMEM((2, 32, 8, C), F32),
-            pltpu.SemaphoreType.DMA((5,)),
+            pltpu.SemaphoreType.DMA((12,)),
             pltpu.SemaphoreType.DMA((2,)),
             pltpu.SemaphoreType.DMA((2,)),
             pltpu.SemaphoreType.DMA((2, 2)),

time: 55.8 us -> 54.6 us (0.978)
  Pallas kernels: 55.5 us -> 54.3 us
    pallas_call x1, Pallas kernels: 52.3 us -> 51.1 us  [body(): pl.pallas_call(kernel, out_shape=[pltpu.VMEM((TILE * TILE, C), F32), pltp...]
where the time goes in v5:
time: 54.6 us; the launch traced here: 54.5 us
  Pallas kernels  54.3 us (99%)
    pallas_call x1, Pallas kernels, body(): pl.pallas_call(kernel, out_shape=[pltpu.VMEM((TILE * TILE, C), F32), pltp...  51.1 us
    pallas_call x1, Pallas kernels, body(): pl.pallas_call(result_kernel, out_shape=jax.ShapeDtypeStruct((TILE, TILE,...  3.17 us

profile of v5, /device:TPU:1, one launch (start us, length us, event | category | flops | bytes accessed | tf_op | source)
XLA Modules:
  0.0 54.5 jit_solution(6475304404242970064)
XLA Ops:
  0.0 51.1 %block.1 = (f32[16384,128]{1,0:T(8,128)S(1)}, bf16[128,128,128]{2,1,0:T(8,128)(2,1)S(1)}, f32[8,128]{1,0:T(8,128)S(1)}) custom-call(bf16[128,128,128]{2,1,0:T(8,128)(2,1)} %bitcast.11, f32[256,640]{1,0:T(8,128)} %cells_hbm.1, f32[640,128]{1,0:T(8,128)} %proj_hbm.1, bf16[3,3,128,128]{3,2,1,0:T(8,128)(2,1)} %k1_hbm.1, bf16[3,3,128,128]{3,2,1,0:T(8,128)(2,1)} %k2_hbm.1, ...), custom_call_target="tpu_custom_call" | custom-call | tf_op jit(solution)/shard_map/block/pallas_call | solution.py:653
  51.1 3.2 %result.1 = bf16[128,128,128]{2,1,0:T(8,128)(2,1)} custom-call(f32[16384,128]{1,0:T(8,128)S(1)} %get-tuple-element.8.field, bf16[128,128,128]{2,1,0:T(8,128)(2,1)S(1)} %get-tuple-element.9.mixed, f32[8,128]{1,0:T(8,128)S(1)} %get-tuple-element.10.terms), custom_call_target="tpu_custom_call" | custom-call | tf_op jit(solution)/shard_map/result/pallas_call | solution.py:727

commit v6 on v5

--- a/solution.py
+++ b/solution.py
@@ -163,7 +163,8 @@
         pl.semaphore_signal(barrier, inc=1, device_id=me ^ far_first(n), device_id_type=FLAT)
         return c
 
-    lax.fori_loop(0, 127, greet, 0)
+    lax.fori_loop(0, 126, greet, 0, unroll=6)
+    greet(126, 0)
     for c in loads[:5] + loads[6:]:
         c.start()
     loads[5].wait()
@@ -181,7 +182,8 @@
         ).start()
         return c
 
-    lax.fori_loop(0, 127, send_ids, 0)
+    lax.fori_loop(0, 126, send_ids, 0, unroll=6)
+    send_ids(126, 0)
 
     for n in (0, 1, 6, 7, 8, 9, 10, 11):
         loads[n].wait()
@@ -270,16 +272,16 @@
 
     lax.fori_loop(0, 8, reorder, 0)
 
-    def conv_block(x, wb, t):
-        y = t * (2 * PAIRS)
+    def conv_block(x, wb, t, pairs=PAIRS):
+        y = t * (2 * pairs)
         lhs = []
-        for q in range(PAIRS):
+        for q in range(pairs):
             parts = [
                 x[y + 2 * q + a, b * 16 : b * 16 + 128] for a in range(4) for b in range(3)
             ]
             lhs.append(jnp.concatenate(parts, axis=1))
         got = jnp.dot(jnp.concatenate(lhs, axis=0), wb[...], preferred_element_type=F32)
-        for q in range(PAIRS):
+        for q in range(pairs):
             for e in range(2):
                 yield y + 2 * q + e, got[q * 128 : (q + 1) * 128, e * 128 : (e + 1) * 128]
 
@@ -287,7 +289,7 @@
         return pl.ds(pl.multiple_of(h * 128, 128), 128)
 
     def conv_noisy(t, c):
-        for h, v in conv_block(x2, wb1, t):
+        for h, v in conv_block(x2, wb1, t, 32):
             field[at_row(h), :] = v
         return c
 
@@ -318,8 +320,9 @@
         ).start()
         return c
 
-    lax.fori_loop(0, 127, send_rows, 0)
-    lax.fori_loop(0, 64 // PAIRS, conv_noisy, 0)
+    lax.fori_loop(0, 126, send_rows, 0, unroll=6)
+    send_rows(126, 0)
+    lax.fori_loop(0, 2, conv_noisy, 0)
     whole(id_buf.at[pl.ds(1, 127)], id_sem.at[0]).wait()
     whole(rows_in.at[pl.ds(1, 127)], row_sem.at[1]).wait()
 
@@ -558,7 +561,8 @@
             ).start()
             return c
 
-        lax.fori_loop(96, 127, send, 0)
+        for t in range(96, 127):
+            send(t, 0)
         if meanwhile is not None:
             meanwhile()
         whole(st_in.at[n, pl.ds(1, 31)], st_sem.at[n, 1]).wait()

time: 54.6 us -> 53.4 us (0.978)
  Pallas kernels: 54.3 us -> 53.2 us
    pallas_call x1, Pallas kernels: 51.1 us -> 50 us  [body(): pl.pallas_call(kernel, out_shape=[pltpu.VMEM((TILE * TILE, C), F32), pltp...]
where the time goes in v6:
time: 53.4 us; the launch traced here: 53.3 us
  Pallas kernels  53.2 us (100%)
    pallas_call x1, Pallas kernels, body(): pl.pallas_call(kernel, out_shape=[pltpu.VMEM((TILE * TILE, C), F32), pltp...  50 us
    pallas_call x1, Pallas kernels, body(): pl.pallas_call(result_kernel, out_shape=jax.ShapeDtypeStruct((TILE, TILE,...  3.17 us

profile of v6, /device:TPU:1, one launch (start us, length us, event | category | flops | bytes accessed | tf_op | source)
XLA Modules:
  0.0 53.3 jit_solution(15831800806830164356)
XLA Ops:
  0.0 50.0 %block.1 = (f32[16384,128]{1,0:T(8,128)S(1)}, bf16[128,128,128]{2,1,0:T(8,128)(2,1)S(1)}, f32[8,128]{1,0:T(8,128)S(1)}) custom-call(bf16[128,128,128]{2,1,0:T(8,128)(2,1)} %bitcast.11, f32[256,640]{1,0:T(8,128)} %cells_hbm.1, f32[640,128]{1,0:T(8,128)} %proj_hbm.1, bf16[3,3,128,128]{3,2,1,0:T(8,128)(2,1)} %k1_hbm.1, bf16[3,3,128,128]{3,2,1,0:T(8,128)(2,1)} %k2_hbm.1, ...), custom_call_target="tpu_custom_call" | custom-call | tf_op jit(solution)/shard_map/block/pallas_call | solution.py:657
  50.0 3.2 %result.1 = bf16[128,128,128]{2,1,0:T(8,128)(2,1)} custom-call(f32[16384,128]{1,0:T(8,128)S(1)} %get-tuple-element.8.field, bf16[128,128,128]{2,1,0:T(8,128)(2,1)S(1)} %get-tuple-element.9.mixed, f32[8,128]{1,0:T(8,128)S(1)} %get-tuple-element.10.terms), custom_call_target="tpu_custom_call" | custom-call | tf_op jit(solution)/shard_map/result/pallas_call | solution.py:731

commit v7 on v6

--- a/solution.py
+++ b/solution.py
@@ -163,7 +163,7 @@
         pl.semaphore_signal(barrier, inc=1, device_id=me ^ far_first(n), device_id_type=FLAT)
         return c
 
-    lax.fori_loop(0, 126, greet, 0, unroll=6)
+    lax.fori_loop(0, 126, greet, 0, unroll=18)
     greet(126, 0)
     for c in loads[:5] + loads[6:]:
         c.start()
@@ -182,7 +182,7 @@
         ).start()
         return c
 
-    lax.fori_loop(0, 126, send_ids, 0, unroll=6)
+    lax.fori_loop(0, 126, send_ids, 0, unroll=18)
     send_ids(126, 0)
 
     for n in (0, 1, 6, 7, 8, 9, 10, 11):
@@ -320,7 +320,7 @@
         ).start()
         return c
 
-    lax.fori_loop(0, 126, send_rows, 0, unroll=6)
+    lax.fori_loop(0, 126, send_rows, 0, unroll=18)
     send_rows(126, 0)
     lax.fori_loop(0, 2, conv_noisy, 0)
     whole(id_buf.at[pl.ds(1, 127)], id_sem.at[0]).wait()

time: 53.4 us -> 53.4 us (level)
  no operation moved by 1% of the time
where the time goes in v7:
time: 53.4 us; the launch traced here: 53.3 us
  Pallas kernels  53.1 us (99%)
    pallas_call x1, Pallas kernels, body(): pl.pallas_call(kernel, out_shape=[pltpu.VMEM((TILE * TILE, C), F32), pltp...  49.9 us
    pallas_call x1, Pallas kernels, body(): pl.pallas_call(result_kernel, out_shape=jax.ShapeDtypeStruct((TILE, TILE,...  3.17 us

profile of v7, /device:TPU:1, one launch (start us, length us, event | category | flops | bytes accessed | tf_op | source)
XLA Modules:
  0.0 53.3 jit_solution(14781314192258947832)
XLA Ops:
  0.0 49.9 %block.1 = (f32[16384,128]{1,0:T(8,128)S(1)}, bf16[128,128,128]{2,1,0:T(8,128)(2,1)S(1)}, f32[8,128]{1,0:T(8,128)S(1)}) custom-call(bf16[128,128,128]{2,1,0:T(8,128)(2,1)} %bitcast.11, f32[256,640]{1,0:T(8,128)} %cells_hbm.1, f32[640,128]{1,0:T(8,128)} %proj_hbm.1, bf16[3,3,128,128]{3,2,1,0:T(8,128)(2,1)} %k1_hbm.1, bf16[3,3,128,128]{3,2,1,0:T(8,128)(2,1)} %k2_hbm.1, ...), custom_call_target="tpu_custom_call" | custom-call | tf_op jit(solution)/shard_map/block/pallas_call | solution.py:657
  49.9 3.2 %result.1 = bf16[128,128,128]{2,1,0:T(8,128)(2,1)} custom-call(f32[16384,128]{1,0:T(8,128)S(1)} %get-tuple-element.8.field, bf16[128,128,128]{2,1,0:T(8,128)(2,1)S(1)} %get-tuple-element.9.mixed, f32[8,128]{1,0:T(8,128)S(1)} %get-tuple-element.10.terms), custom_call_target="tpu_custom_call" | custom-call | tf_op jit(solution)/shard_map/result/pallas_call | solution.py:731
